TPU v7x, 32 devices: a whole 2x2x4 slice. The times are simulated.
32 devices in a mesh: gz: 16 (over z, x, core), ph: 2 (over y).
Axes of the slice: x: 2, y: 2, z: 4, core: 2. Of those that a mesh axis runs over, the one named last changes fastest.
Arguments:
- frac: bfloat16 [2, 128, 64, 256], P('ph', 'gz'), may hold values from 0.0099487305 to 0.099609375
- velocity: bfloat16 [2, 3, 128, 64, 256], P('ph', None, 'gz'), may hold values from -6 to 6
- gas_vel: bfloat16 [3, 128, 64, 256], P(None, 'gz'), may hold values from -6 to 6
- diameters: float32 [32], replicated, may hold values from 0.5 to 4
- phase_map: int32 [2], P('ph'), may hold values from 0 to 31
- wall_mask: int32 [64, 256], replicated, may hold values 0 or 1
- offsets: int32 [128], replicated, may hold values from 0 to 255
Outputs:
- pressure: float32 [128, 64, 256], P('gz')
- corrected: bfloat16 [2, 3, 128, 64, 256], P('ph', None, 'gz')
Inputs may be any that keep to these rules, and one draw needn't show every extreme that they name: `wall_mask`: 1 marks a fluid cell, 0 a lifter or wall cell.
All inputs are finite; a program needn't handle non-finite values.
Results may differ from a plain program's by a relative error of at most 0.001.
Values sent between devices are 32-bit elements; how exact they have to be, the bound alone decides.
A program may use at most 64 MiB of HBM per device.

v0:
```python
import functools
import math

import jax
import jax.numpy as jnp
import numpy as np
from jax import lax
from jax.experimental import pallas as pl
from jax.experimental.pallas import tpu as pltpu
from jax.sharding import PartitionSpec as P

DT_STEP = 0.5
DRAG_SCALE = 20.0
COMPRESS = 0.005
CORRECT_STEPS = 2
HIGHEST = lax.Precision.HIGHEST


def from_behind(block, axis, distance):
    devices = range(lax.axis_size(axis))
    route = [((i - distance) % len(devices), i) for i in devices]
    return lax.ppermute(block, axis, route)


def real_basis(count):
    index_rows = jnp.arange(count, dtype=jnp.int32)[:, None]
    column = jnp.arange(count, dtype=jnp.int32)[None, :]
    half = count // 2
    wave = jnp.where(column <= half, column, column - half)
    angle = 2.0 * math.pi / count * (index_rows * wave % count).astype(jnp.float32)
    scaled = math.sqrt(2.0 / count)
    cosine = jnp.cos(angle)
    table = jnp.where(column < half, scaled * cosine, scaled * jnp.sin(angle))
    return jnp.where((column == 0) | (column == half), cosine / math.sqrt(count), table)


def eigen_values(count):
    column = jnp.arange(count, dtype=jnp.int32)
    half = count // 2
    wave = jnp.where(column <= half, column, column - half).astype(jnp.float32)
    return 2.0 - 2.0 * jnp.cos(2.0 * math.pi / count * wave)


def rotate_mask(wall_mask, turns, around_count):
    around_idx = (
        jnp.arange(around_count, dtype=jnp.int32)[None, :] - turns[:, None]
    ) % around_count
    return jnp.transpose(jnp.take(wall_mask, around_idx, axis=1), (1, 0, 2)).astype(jnp.float32)


def radial_solve(spectral, axial_eig, theta_eig, radius_vec, angle_step):
    radial_count = radius_vec.shape[0]
    inner = radius_vec - 0.5
    outer = jnp.where(jnp.arange(radial_count) == radial_count - 1, 0.0, radius_vec + 0.5)
    diag = (
        COMPRESS
        + axial_eig[:, None, None]
        + theta_eig[None, :, None] / (radius_vec * angle_step) ** 2
        + ((outer + inner) / radius_vec)[None, None, :]
    )
    lower = jnp.broadcast_to(-inner / radius_vec, diag.shape)
    upper = jnp.broadcast_to(-outer / radius_vec, diag.shape)
    right = -jnp.transpose(spectral, (0, 2, 1))[..., None]
    solved = lax.linalg.tridiagonal_solve(lower, diag, upper, right)[..., 0]
    return jnp.transpose(solved, (0, 2, 1))


def to_space(modes, around_table):
    return jnp.dot(
        modes.reshape(-1, around_table.shape[0]), around_table.T, precision=HIGHEST
    ).reshape(modes.shape)


def shards(frac, velocity, gas_vel, diameters, phase_map, wall_mask, offsets):
    plane_count = frac.shape[1]
    radial_count = frac.shape[2]
    around_count = frac.shape[3]
    axial_total = offsets.shape[0]
    phase_count = lax.axis_size("ph")
    slab_index = lax.axis_index("gz")
    first_plane = slab_index * plane_count
    angle_step = 2.0 * math.pi / around_count
    plane_ids = (first_plane + jnp.arange(plane_count + 1, dtype=jnp.int32)) % axial_total
    fluid_all = rotate_mask(wall_mask, jnp.take(offsets, plane_ids), around_count)
    fluid = fluid_all[:plane_count]
    open_radial = fluid * jnp.concatenate([fluid[:, 1:], jnp.zeros_like(fluid[:, :1])], 1)
    open_around = fluid * jnp.roll(fluid, -1, 2)
    open_axial = fluid * fluid_all[1:]
    radius_vec = jnp.arange(radial_count, dtype=jnp.float32) + 0.5
    radii = radius_vec[:, None]
    which = (jnp.arange(diameters.shape[0], dtype=jnp.int32) == phase_map[0]).astype(jnp.float32)
    size_here = jnp.sum(diameters * which)
    volume = frac[0].astype(jnp.float32)
    gas = gas_vel.astype(jnp.float32)
    slip = velocity[0].astype(jnp.float32) - gas
    speed = jnp.sqrt(1.0 + jnp.sum(slip * slip, 0))
    beta = DRAG_SCALE * volume / (size_here * size_here) * (1.0 + 0.15 * speed)
    relax = 1.0 / (1.0 + DT_STEP * beta)
    predicted = gas + relax * slip
    share = volume * relax * slip + gas / phase_count
    flux_radial = share[0] * open_radial
    flux_around = share[1] * open_around
    flux_axial = share[2] * open_axial
    below = from_behind(flux_axial[-1:], "gz", 1)
    axial_prev = jnp.concatenate([below, flux_axial[:-1]], 0)
    radial_prev = jnp.concatenate([jnp.zeros_like(flux_radial[:, :1]), flux_radial[:, :-1]], 1)
    term = ((radii + 0.5) * flux_radial - (radii - 0.5) * radial_prev) / radii
    term = term + (flux_around - jnp.roll(flux_around, 1, 2)) / (radii * angle_step)
    term = (term + flux_axial - axial_prev) / DT_STEP
    around_table = real_basis(around_count)
    axial_table = real_basis(axial_total)
    axial_eig = eigen_values(axial_total)
    axial_step = None
    source = lax.psum(term, "ph")
    modes = jnp.dot(source.reshape(-1, around_count), around_table, precision=HIGHEST).reshape(
        source.shape
    )
    pencil = lax.all_to_all(modes, "gz", split_axis=2, concat_axis=0, tiled=True)
    mode_count = pencil.shape[2]
    theta_eig = lax.dynamic_slice_in_dim(
        eigen_values(around_count), slab_index * mode_count, mode_count
    )
    flat = pencil.reshape(axial_total, -1)
    spectral = jnp.dot(axial_table.T, flat, precision=HIGHEST).reshape(pencil.shape)
    solved = radial_solve(spectral, axial_eig, theta_eig, radius_vec, angle_step)
    space = jnp.dot(axial_table, solved.reshape(axial_total, -1), precision=HIGHEST).reshape(
        pencil.shape
    )
    ahead = jnp.roll(space, -1, 0) - space
    back, back_step = (
        lax.all_to_all(space, "gz", split_axis=0, concat_axis=2, tiled=True),
        lax.all_to_all(ahead, "gz", split_axis=0, concat_axis=2, tiled=True),
    )
    pressure = to_space(back, around_table)
    axial_step = to_space(back_step, around_table)
    radial_step = (jnp.concatenate([pressure[:, 1:], pressure[:, -1:]], 1) - pressure) * open_radial
    around_step = (jnp.roll(pressure, -1, 2) - pressure) / (radii * angle_step) * open_around
    gradient = jnp.stack([radial_step, around_step, axial_step * open_axial])
    corrected = (predicted - DT_STEP * gradient).astype(jnp.bfloat16)[None]
    return (pressure, corrected)


MESH_ID = pl.DeviceIdType.MESH


def split_low(x):
    high = x.astype(jnp.bfloat16)
    return high, (x - high.astype(jnp.float32)).astype(jnp.bfloat16)


def triple_dot(x, table_high, table_low):
    high, low = split_low(x)
    out = jnp.dot(high, table_high, preferred_element_type=jnp.float32)
    out = out + jnp.dot(low, table_high, preferred_element_type=jnp.float32)
    return out + jnp.dot(high, table_low, preferred_element_type=jnp.float32)


def np_high_low(table):
    high = table.astype(jnp.bfloat16)
    low = (table - high.astype(np.float64)).astype(jnp.bfloat16)
    return high, low


@functools.lru_cache(maxsize=None)
def operator_tables(radial, around, axial, planes):
    half = around // 2
    rows = np.arange(around)[:, None]
    column = np.arange(around)[None, :]
    wave = np.where(column <= half, column, column - half)
    angle = 2.0 * np.pi / around * (rows * wave % around)
    basis = np.sqrt(2.0 / around) * np.where(column <= half, np.cos(angle), np.sin(angle))
    basis = np.where((column == 0) | (column == half), np.cos(angle) / np.sqrt(around), basis)
    radius = np.arange(radial) + 0.5
    inner = radius - 0.5
    outer = np.where(np.arange(radial) == radial - 1, 0.0, radius + 0.5)
    step = 2.0 * np.pi / around
    vectors, values = [], []
    for m in range(half + 1):
        eig = 2.0 - 2.0 * np.cos(2.0 * np.pi / around * m)
        matrix = np.diag((outer + inner) / radius + eig / (radius * step) ** 2)
        off = -outer[:-1] / np.sqrt(radius[:-1] * radius[1:])
        matrix = matrix + np.diag(off, 1) + np.diag(off, -1)
        value, vector = np.linalg.eigh(matrix)
        vector = vector * np.where(vector[:1] < 0.0, -1.0, 1.0)
        values.append(value)
        vectors.append(vector)
    vectors = np.stack(vectors, -1)
    values = np.maximum(np.stack(values, -1), 0.0)
    first = vectors[:, :, :half]
    nyquist = np.zeros((radial, max(radial, 128)))
    nyquist[:, :radial] = vectors[:, :, half].T
    other = np.concatenate([values[:, half:], values[:, 1:half]], -1)
    over = COMPRESS + np.stack([values[:, :half], other])
    root = np.sqrt(over * (over + 4.0))
    ratio = 2.0 / (2.0 + over + root)
    jump = ratio**planes
    wrap = 1.0 / (1.0 - ratio**axial)
    line = np.stack([ratio, 1.0 / root, jump, wrap], 1).astype(np.float32)
    ahead = np_high_low(basis)
    back = np_high_low(basis.T.copy())
    return (
        first.astype(np.float32),
        nyquist.astype(np.float32),
        line,
        np.stack(ahead),
        np.stack(back),
    )


def drum_kernel(
    gz_count,
    offsets_ref,
    diameters_ref,
    map_ref,
    wall_hbm,
    frac_hbm,
    velocity_hbm,
    gas_hbm,
    ahead_hbm,
    nyquist_hbm,
    line_hbm,
    back_hbm,
    radial_hbm,
    space_out,
    pred_out,
    fluid_out,
    wall_ref,
    frac_ref,
    velocity_ref,
    gas_ref,
    ahead_ref,
    nyquist_ref,
    line_ref,
    back_ref,
    fluid,
    pred,
    term,
    axial_flux,
    halo,
    modes,
    partner,
    radial,
    radial_back,
    lines,
    ends_out,
    ends_in,
    states_out,
    states_in,
    solved,
    result,
    space,
    table_sem,
    input_sem,
    out_sem,
    halo_sem,
    swap_send,
    swap_recv,
    ends_send,
    ends_recv,
    states_send,
    states_recv,
    back_send,
    back_recv,
):
    me = lax.axis_index("gz")
    ph = lax.axis_index("ph")
    other = 1 - ph
    planes, rows, around = term.shape
    half = around // 2
    axial_total = offsets_ref.shape[0]
    blocks = rows // 8
    angle_step = 2.0 * math.pi / around

    barrier = pltpu.get_barrier_semaphore()
    for hop in range(1, gz_count):
        pl.semaphore_signal(
            barrier, inc=1, device_id=(lax.rem(me + hop, gz_count), ph), device_id_type=MESH_ID
        )
    pl.semaphore_signal(barrier, inc=1, device_id=(me, other), device_id_type=MESH_ID)

    pairs = (
        (wall_hbm, wall_ref),
        (frac_hbm, frac_ref),
        (velocity_hbm, velocity_ref),
        (gas_hbm, gas_ref),
        (ahead_hbm, ahead_ref),
        (nyquist_hbm, nyquist_ref),
        (line_hbm, line_ref),
        (back_hbm, back_ref),
    )
    fetches = [pltpu.make_async_copy(a, b, input_sem.at[i]) for i, (a, b) in enumerate(pairs)]
    table_copy = pltpu.make_async_copy(radial_hbm, radial, table_sem)
    for fetch in fetches[:5]:
        fetch.start()
    table_copy.start()
    for fetch in fetches[5:]:
        fetch.start()
    fluid_copy = pltpu.make_async_copy(fluid, fluid_out, out_sem.at[0])
    pred_copy = pltpu.make_async_copy(pred, pred_out, out_sem.at[1])
    fetches[0].wait()

    radii = lax.broadcasted_iota(jnp.int32, (rows, around), 0).astype(jnp.float32) + 0.5
    row_id = lax.broadcasted_iota(jnp.int32, (rows, around), 0)
    wall = wall_ref[...].astype(jnp.float32).astype(jnp.bfloat16)
    from_col = lax.broadcasted_iota(jnp.int32, (around, around), 0)
    to_col = lax.broadcasted_iota(jnp.int32, (around, around), 1)
    gap = to_col - from_col

    def rotate(z, carry):
        turn = offsets_ref[lax.rem(me * planes + z, axial_total)]
        hit = (gap == turn) | (gap == turn - around)
        one_hot = jnp.where(hit, 1.0, 0.0).astype(jnp.bfloat16)
        fluid[z] = jnp.dot(wall, one_hot, preferred_element_type=jnp.float32)
        return carry

    lax.fori_loop(0, planes + 1, rotate, 0)

    fluid_copy.start()
    for fetch in fetches[1:4]:
        fetch.wait()
    size = diameters_ref[map_ref[0]]
    axial_flux[0] = jnp.zeros((rows, around), jnp.float32)

    def opens(z):
        here = fluid[z]
        open_radial = jnp.where(row_id == rows - 1, 0.0, here * pltpu.roll(here, rows - 1, 0))
        open_around = here * pltpu.roll(here, around - 1, 1)
        return open_radial, open_around, here * fluid[z + 1]

    weight = -jnp.sqrt(radii) / DT_STEP
    share = 1.0 / lax.axis_size("ph")

    def source(z, carry):
        volume = frac_ref[0, z].astype(jnp.float32)
        gas = [gas_ref[a, z].astype(jnp.float32) for a in range(3)]
        slip = [velocity_ref[0, a, z].astype(jnp.float32) - gas[a] for a in range(3)]
        speed = jnp.sqrt(1.0 + (slip[0] * slip[0] + slip[1] * slip[1] + slip[2] * slip[2]))
        beta = DRAG_SCALE * volume / (size * size) * (1.0 + 0.15 * speed)
        relax = 1.0 / (1.0 + DT_STEP * beta)
        open_radial, open_around, open_axial = opens(z)
        for a in range(3):
            pred[a, z] = gas[a] + relax * slip[a]
        pull = volume * relax
        flux_radial = (pull * slip[0] + share * gas[0]) * open_radial
        flux_around = (pull * slip[1] + share * gas[1]) * open_around
        flux_axial = (pull * slip[2] + share * gas[2]) * open_axial
        axial_flux[z + 1] = flux_axial
        out = (radii + 0.5) * flux_radial
        inward = jnp.where(row_id == 0, 0.0, pltpu.roll(out, 1, 0))
        total = (out - inward) / radii
        total = total + (flux_around - pltpu.roll(flux_around, 1, 1)) / (radii * angle_step)
        term[z] = (total + flux_axial - axial_flux[z]) * weight
        return carry

    lax.fori_loop(0, planes, source, 0)

    pred_copy.start()
    fetches[4].wait()
    pl.semaphore_wait(barrier, gz_count)

    halo_copy = pltpu.make_async_remote_copy(
        src_ref=axial_flux.at[planes],
        dst_ref=halo,
        send_sem=halo_sem.at[0],
        recv_sem=halo_sem.at[1],
        device_id=(lax.rem(me + 1, gz_count), ph),
        device_id_type=MESH_ID,
    )
    halo_copy.start()

    def swap(z):
        return pltpu.make_async_remote_copy(
            src_ref=modes.at[other, z],
            dst_ref=partner.at[z],
            send_sem=swap_send.at[z],
            recv_sem=swap_recv.at[z],
            device_id=(me, other),
            device_id_type=MESH_ID,
        )

    def to_modes(z, value):
        out = triple_dot(value, ahead_ref[0], ahead_ref[1])
        modes[0, z] = out[:, :half]
        modes[1, z] = out[:, half:]
        swap(z).start()

    def send_modes(k, carry):
        to_modes(k, term[k])
        return carry

    lax.fori_loop(1, planes, send_modes, 0)
    halo_copy.wait()
    to_modes(0, term[0] - halo[...] * weight)

    table_copy.wait()
    for fetch in fetches[5:]:
        fetch.wait()
    is_other = jnp.where(ph == 1, 1, 0)
    lane0 = (lax.broadcasted_iota(jnp.int32, (rows, half), 1) == 0) & (
        jnp.broadcast_to(is_other, (rows, half)) == 1
    )
    for r in range(rows):
        fill = jnp.broadcast_to(nyquist_ref[:, r : r + 1], (rows, half))
        radial[pl.ds(r * rows, rows), :] = jnp.where(lane0, fill, radial[pl.ds(r * rows, rows), :])

    def apply(table, load, z):
        def add(k, acc):
            for j in range(8):
                r = k * 8 + j
                line = jnp.broadcast_to(load(z, r), (rows, half))
                acc = acc + table[pl.ds(pl.multiple_of(r * rows, rows), rows), :] * line
            return acc

        return lax.fori_loop(0, rows // 8, add, jnp.zeros((rows, half), jnp.float32))

    def load_term(z, r):
        return modes[ph, z, pl.ds(r, 1), :] + partner[z, pl.ds(r, 1), :]

    def forward(k, carry):
        z = lax.rem(k + 1, planes)
        swap(z).wait_recv()
        lines[z] = apply(radial, load_term, z)
        return carry

    lax.fori_loop(0, planes, forward, 0)

    ratio = line_ref[ph, 0]
    rising = lines[0]
    for z in range(1, planes):
        rising = rising * ratio + lines[z]
    falling = lines[planes - 1]
    for z in range(planes - 2, -1, -1):
        falling = falling * ratio + lines[z]
    for j in range(blocks):
        ends_out[j] = rising[8 * j : 8 * j + 8]
        ends_out[blocks + j] = falling[8 * j : 8 * j + 8]

    def exchange(src, dst, send, recv, hop, sender):
        to = lax.rem(me + hop, gz_count)
        at = lax.rem(me + gz_count - hop, gz_count) if sender else me
        return pltpu.make_async_remote_copy(
            src_ref=src.at[to],
            dst_ref=dst.at[at],
            send_sem=send.at[hop],
            recv_sem=recv.at[hop],
            device_id=(to, ph),
            device_id_type=MESH_ID,
        )

    for hop in range(1, gz_count):
        exchange(ends_out, ends_in, ends_send, ends_recv, hop, False).start()
    ends_in[me] = ends_out[me]

    def flip(l, carry):
        radial_back[pl.ds(pl.multiple_of(l * rows, rows), rows), :] = radial[
            pl.ds(l, rows, stride=rows), :
        ]
        return carry

    lax.fori_loop(0, rows, flip, 0)

    for hop in range(1, gz_count):
        exchange(ends_out, ends_in, ends_send, ends_recv, hop, True).wait_recv()

    is_rise = 1 - me // blocks
    mine = lax.rem(me, blocks)
    jump = line_ref[ph, 2, pl.ds(pl.multiple_of(mine * 8, 8), 8), :]
    wrap = line_ref[ph, 3, pl.ds(pl.multiple_of(mine * 8, 8), 8), :]
    order = [is_rise * s + (1 - is_rise) * (gz_count - 1 - s) for s in range(gz_count)]
    state = jnp.zeros((8, half), jnp.float32)
    for s in range(gz_count):
        state = state * jump + ends_in[order[s]]
    state = state * wrap
    for s in range(gz_count):
        states_out[order[s]] = state
        state = state * jump + ends_in[order[s]]

    for hop in range(1, gz_count):
        exchange(states_out, states_in, states_send, states_recv, hop, False).start()
    states_in[me] = states_out[me]
    for hop in range(1, gz_count):
        exchange(states_out, states_in, states_send, states_recv, hop, True).wait_recv()

    scale = line_ref[ph, 1]
    right = jnp.concatenate([states_in[blocks + j] for j in range(blocks)], 0)
    left = jnp.concatenate([states_in[j] for j in range(blocks)], 0)
    solved[planes] = right
    behind = right * ratio
    for z in range(planes - 1, -1, -1):
        solved[z] = behind
        behind = (behind + lines[z]) * ratio
    ahead_state = left
    for z in range(planes):
        ahead_state = ahead_state * ratio + lines[z]
        solved[z] = (solved[z] + ahead_state) * scale
    solved[planes] = (solved[planes] + ahead_state * ratio) * scale

    def give(z, index):
        return pltpu.make_async_remote_copy(
            src_ref=result.at[index, z],
            dst_ref=result.at[index, z],
            send_sem=back_send.at[z],
            recv_sem=back_recv.at[z],
            device_id=(me, other),
            device_id_type=MESH_ID,
        )

    def load_solved(z, r):
        return solved[z, pl.ds(r, 1), :]

    shrink = 1.0 / jnp.sqrt(radii[:, :half])

    def inverse(z, carry):
        result[ph, z] = apply(radial_back, load_solved, z) * shrink
        give(z, ph).start()
        return carry

    lax.fori_loop(0, planes + 1, inverse, 0)

    def finish(z, carry):
        give(z, other).wait_recv()
        both = jnp.concatenate([result[0, z], result[1, z]], 1)
        space[z] = triple_dot(both, back_ref[0], back_ref[1])
        pltpu.make_async_copy(space.at[z], space_out.at[z], out_sem.at[z + 2]).start()
        return carry

    lax.fori_loop(0, planes + 1, finish, 0)

    for z in range(planes):
        swap(z).wait_send()
    for hop in range(1, gz_count):
        exchange(ends_out, ends_in, ends_send, ends_recv, hop, False).wait_send()
        exchange(states_out, states_in, states_send, states_recv, hop, False).wait_send()
    for z in range(planes + 1):
        give(z, ph).wait_send()
        pltpu.make_async_copy(space.at[z], space_out.at[z], out_sem.at[z + 2]).wait()
    fluid_copy.wait()
    pred_copy.wait()


def correct_kernel(space, space_next, pred, fluid, fluid_next, pressure_ref, corrected_ref):
    count, rows, around = space.shape
    radii = lax.broadcasted_iota(jnp.int32, (rows, around), 0).astype(jnp.float32) + 0.5
    row_id = lax.broadcasted_iota(jnp.int32, (rows, around), 0)
    angle_step = 2.0 * math.pi / around
    arc = 1.0 / (radii * angle_step)
    for z in range(count):
        here = space[z]
        mask = fluid[z]
        space_later = space[z + 1] if z + 1 < count else space_next[0]
        mask_later = fluid[z + 1] if z + 1 < count else fluid_next[0]
        pressure_ref[z] = here
        open_radial = jnp.where(row_id == rows - 1, 0.0, mask * pltpu.roll(mask, rows - 1, 0))
        open_around = mask * pltpu.roll(mask, around - 1, 1)
        radial_step = (pltpu.roll(here, rows - 1, 0) - here) * open_radial
        around_step = (pltpu.roll(here, around - 1, 1) - here) * arc * open_around
        axial_step = (space_later - here) * (mask * mask_later)
        for a, step in enumerate((radial_step, around_step, axial_step)):
            corrected_ref[0, a, z] = (pred[a, z] - DT_STEP * step).astype(jnp.bfloat16)


def drum_step(gz_count, frac, velocity, gas_vel, diameters, phase_map, wall_mask, offsets):
    planes, rows, around = frac.shape[1:]
    half = around // 2
    first, nyquist, line, ahead, back = operator_tables(rows, around, offsets.shape[0], planes)
    smem = pl.BlockSpec(memory_space=pltpu.SMEM)
    f32 = jnp.float32
    dma = pltpu.SemaphoreType.DMA
    ends = (gz_count, 8, half)
    space, pred, fluid = pl.pallas_call(
        functools.partial(drum_kernel, gz_count),
        out_shape=(
            jax.ShapeDtypeStruct((planes + 1, rows, around), f32),
            jax.ShapeDtypeStruct((3, planes, rows, around), f32),
            jax.ShapeDtypeStruct((planes + 1, rows, around), f32),
        ),
        in_specs=[smem] * 3 + [pl.BlockSpec(memory_space=pl.ANY)] * 9,
        out_specs=[pl.BlockSpec(memory_space=pl.ANY)] * 3,
        scratch_shapes=[
            pltpu.VMEM(wall_mask.shape, jnp.int32),
            pltpu.VMEM(frac.shape, jnp.bfloat16),
            pltpu.VMEM(velocity.shape, jnp.bfloat16),
            pltpu.VMEM(gas_vel.shape, jnp.bfloat16),
            pltpu.VMEM(ahead.shape, jnp.bfloat16),
            pltpu.VMEM(nyquist.shape, f32),
            pltpu.VMEM(line.shape, f32),
            pltpu.VMEM(back.shape, jnp.bfloat16),
            pltpu.VMEM((planes + 1, rows, around), f32),
            pltpu.VMEM((3, planes, rows, around), f32),
            pltpu.VMEM((planes, rows, around), f32),
            pltpu.VMEM((planes + 1, rows, around), f32),
            pltpu.VMEM((rows, around), f32),
            pltpu.VMEM((2, planes, rows, half), f32),
            pltpu.VMEM((planes, rows, half), f32),
            pltpu.VMEM((rows * rows, half), f32),
            pltpu.VMEM((rows * rows, half), f32),
            pltpu.VMEM((planes, rows, half), f32),
            pltpu.VMEM(ends, f32),
            pltpu.VMEM(ends, f32),
            pltpu.VMEM(ends, f32),
            pltpu.VMEM(ends, f32),
            pltpu.VMEM((planes + 1, rows, half), f32),
            pltpu.VMEM((2, planes + 1, rows, half), f32),
            pltpu.VMEM((planes + 1, rows, around), f32),
            dma,
            dma((8,)),
            dma((planes + 3,)),
            dma((2,)),
            dma((planes,)),
            dma((planes,)),
            dma((gz_count,)),
            dma((gz_count,)),
            dma((gz_count,)),
            dma((gz_count,)),
            dma((planes + 1,)),
            dma((planes + 1,)),
        ],
        compiler_params=pltpu.CompilerParams(
            collective_id=0, has_side_effects=True, vmem_limit_bytes=56 * 1024 * 1024
        ),
    )(
        offsets,
        diameters,
        phase_map,
        wall_mask,
        frac,
        velocity,
        gas_vel,
        jnp.asarray(ahead),
        jnp.asarray(nyquist),
        jnp.asarray(line),
        jnp.asarray(back),
        jnp.asarray(first.reshape(rows * rows, half)),
    )
    chunk = planes // CORRECT_STEPS if planes % CORRECT_STEPS == 0 else planes
    here = pl.BlockSpec((chunk, rows, around), lambda k: (k, 0, 0))
    later = pl.BlockSpec((1, rows, around), lambda k: ((k + 1) * chunk, 0, 0))
    return pl.pallas_call(
        correct_kernel,
        grid=(planes // chunk,),
        out_shape=(
            jax.ShapeDtypeStruct((planes, rows, around), f32),
            jax.ShapeDtypeStruct((1, 3, planes, rows, around), jnp.bfloat16),
        ),
        in_specs=[
            here,
            later,
            pl.BlockSpec((3, chunk, rows, around), lambda k: (0, k, 0, 0)),
            here,
            later,
        ],
        out_specs=(here, pl.BlockSpec((1, 3, chunk, rows, around), lambda k: (0, 0, k, 0, 0))),
    )(space, space, pred, fluid, fluid)


def solution(mesh):
    in_specs = (
        P("ph", "gz", None, None),
        P("ph", None, "gz", None, None),
        P(None, "gz", None, None),
        P(),
        P("ph"),
        P(),
        P(),
    )
    out_specs = (P("gz", None, None), P("ph", None, "gz", None, None))
    gz_count, ph_count = mesh.shape["gz"], mesh.shape["ph"]

    def body(frac, *rest):
        rows, around = frac.shape[2:]
        fits = ph_count == 2 and around == 256 and rows <= 128
        if fits and rows * 2 == gz_count * 8 and frac.shape[1] <= 8:
            return drum_step(gz_count, frac, *rest)
        return shards(frac, *rest)

    return jax.shard_map(body, mesh=mesh, in_specs=in_specs, out_specs=out_specs, check_vma=False)
```

profile of v0, /device:TPU:0, one launch (start us, length us, event | category | flops | bytes accessed | tf_op | source)
XLA Modules:
  0.0 38.8 jit_solution(6539425934327623457)
XLA Ops:
  1.3 34.6 %shard_map.131 = (f32[9,64,256]{2,1,0:T(8,128)}, f32[3,8,64,256]{3,2,1,0:T(8,128)}, f32[9,64,256]{2,1,0:T(8,128)}) custom-call(s32[128]{0:T(128)} %offsets_ref.1, f32[32]{0:T(128)} %diameters_ref.1, s32[1]{0:T(128)S(6)} %copy.14.map_ref, s32[64,256]{1,0:T(8,128)} %wall_hbm.1, bf16[1,8,64,256]{3,2,1,0:T(8,128)(2,1)} %frac_hbm.1, ...), custom_call_target="tpu_custom_call" | custom-call | tf_op jit(solution)/shard_map/pallas_call | solution.py:570
  35.9 2.9 %shard_map.132 = (f32[8,64,256]{2,1,0:T(8,128)}, bf16[1,3,8,64,256]{4,3,2,1,0:T(8,128)(2,1)}) custom-call(f32[9,64,256]{2,1,0:T(8,128)} %get-tuple-element.5.space.space_next, f32[9,64,256]{2,1,0:T(8,128)} %get-tuple-element.5.space.space_next, f32[3,8,64,256]{3,2,1,0:T(8,128)} %get-tuple-element.6.pred, f32[9,64,256]{2,1,0:T(8,128)} %get-tuple-element.7.fluid.fluid_next, ...), custom_call_target="tpu_custom_call" | custom-call | tf_op jit(solution)/shard_map/pallas_call | solution.py:638
where the time goes:
time: 39 us; the launch traced here: 38.8 us
  Pallas kernels  37.5 us (96%)
  between operations  1.29 us (3%)
    pallas_call x1, Pallas kernels, drum_step(): pl.pallas_call(functools.partial(drum_kernel, gz_count), out_shape=(jax.S...  34.6 us
    pallas_call x1, Pallas kernels, drum_step(): pl.pallas_call(correct_kernel, grid=(planes // chunk,), out_shape=(jax.Sh...  2.89 us

commit v1 on v0

--- a/solution.py
+++ b/solution.py
@@ -12,7 +12,6 @@
 DT_STEP = 0.5
 DRAG_SCALE = 20.0
 COMPRESS = 0.005
-CORRECT_STEPS = 2
 HIGHEST = lax.Precision.HIGHEST
 
 
@@ -221,9 +220,8 @@
     line_hbm,
     back_hbm,
     radial_hbm,
-    space_out,
-    pred_out,
-    fluid_out,
+    pressure_ref,
+    corrected_ref,
     wall_ref,
     frac_ref,
     velocity_ref,
@@ -248,10 +246,8 @@
     states_in,
     solved,
     result,
-    space,
     table_sem,
     input_sem,
-    out_sem,
     halo_sem,
     swap_send,
     swap_recv,
@@ -295,8 +291,6 @@
     table_copy.start()
     for fetch in fetches[5:]:
         fetch.start()
-    fluid_copy = pltpu.make_async_copy(fluid, fluid_out, out_sem.at[0])
-    pred_copy = pltpu.make_async_copy(pred, pred_out, out_sem.at[1])
     fetches[0].wait()
 
     radii = lax.broadcasted_iota(jnp.int32, (rows, around), 0).astype(jnp.float32) + 0.5
@@ -315,7 +309,6 @@
 
     lax.fori_loop(0, planes + 1, rotate, 0)
 
-    fluid_copy.start()
     for fetch in fetches[1:4]:
         fetch.wait()
     size = diameters_ref[map_ref[0]]
@@ -354,7 +347,6 @@
 
     lax.fori_loop(0, planes, source, 0)
 
-    pred_copy.start()
     fetches[4].wait()
     pl.semaphore_wait(barrier, gz_count)
 
@@ -517,14 +509,25 @@
 
     lax.fori_loop(0, planes + 1, inverse, 0)
 
-    def finish(z, carry):
+    arc = 1.0 / (radii * angle_step)
+
+    def finish(z):
         give(z, other).wait_recv()
         both = jnp.concatenate([result[0, z], result[1, z]], 1)
-        space[z] = triple_dot(both, back_ref[0], back_ref[1])
-        pltpu.make_async_copy(space.at[z], space_out.at[z], out_sem.at[z + 2]).start()
-        return carry
-
-    lax.fori_loop(0, planes + 1, finish, 0)
+        return triple_dot(both, back_ref[0], back_ref[1])
+
+    def correct(z, here):
+        later = finish(z + 1)
+        pressure_ref[z] = here
+        open_radial, open_around, open_axial = opens(z)
+        radial_step = (pltpu.roll(here, rows - 1, 0) - here) * open_radial
+        around_step = (pltpu.roll(here, around - 1, 1) - here) * arc * open_around
+        axial_step = (later - here) * open_axial
+        for a, step in enumerate((radial_step, around_step, axial_step)):
+            corrected_ref[0, a, z] = (pred[a, z] - DT_STEP * step).astype(jnp.bfloat16)
+        return later
+
+    lax.fori_loop(0, planes, correct, finish(0))
 
     for z in range(planes):
         swap(z).wait_send()
@@ -533,30 +536,6 @@
         exchange(states_out, states_in, states_send, states_recv, hop, False).wait_send()
     for z in range(planes + 1):
         give(z, ph).wait_send()
-        pltpu.make_async_copy(space.at[z], space_out.at[z], out_sem.at[z + 2]).wait()
-    fluid_copy.wait()
-    pred_copy.wait()
-
-
-def correct_kernel(space, space_next, pred, fluid, fluid_next, pressure_ref, corrected_ref):
-    count, rows, around = space.shape
-    radii = lax.broadcasted_iota(jnp.int32, (rows, around), 0).astype(jnp.float32) + 0.5
-    row_id = lax.broadcasted_iota(jnp.int32, (rows, around), 0)
-    angle_step = 2.0 * math.pi / around
-    arc = 1.0 / (radii * angle_step)
-    for z in range(count):
-        here = space[z]
-        mask = fluid[z]
-        space_later = space[z + 1] if z + 1 < count else space_next[0]
-        mask_later = fluid[z + 1] if z + 1 < count else fluid_next[0]
-        pressure_ref[z] = here
-        open_radial = jnp.where(row_id == rows - 1, 0.0, mask * pltpu.roll(mask, rows - 1, 0))
-        open_around = mask * pltpu.roll(mask, around - 1, 1)
-        radial_step = (pltpu.roll(here, rows - 1, 0) - here) * open_radial
-        around_step = (pltpu.roll(here, around - 1, 1) - here) * arc * open_around
-        axial_step = (space_later - here) * (mask * mask_later)
-        for a, step in enumerate((radial_step, around_step, axial_step)):
-            corrected_ref[0, a, z] = (pred[a, z] - DT_STEP * step).astype(jnp.bfloat16)
 
 
 def drum_step(gz_count, frac, velocity, gas_vel, diameters, phase_map, wall_mask, offsets):
@@ -567,15 +546,14 @@
     f32 = jnp.float32
     dma = pltpu.SemaphoreType.DMA
     ends = (gz_count, 8, half)
-    space, pred, fluid = pl.pallas_call(
+    return pl.pallas_call(
         functools.partial(drum_kernel, gz_count),
         out_shape=(
-            jax.ShapeDtypeStruct((planes + 1, rows, around), f32),
-            jax.ShapeDtypeStruct((3, planes, rows, around), f32),
-            jax.ShapeDtypeStruct((planes + 1, rows, around), f32),
+            pltpu.VMEM((planes, rows, around), f32),
+            pltpu.VMEM((1, 3, planes, rows, around), jnp.bfloat16),
         ),
         in_specs=[smem] * 3 + [pl.BlockSpec(memory_space=pl.ANY)] * 9,
-        out_specs=[pl.BlockSpec(memory_space=pl.ANY)] * 3,
+        out_specs=[pl.BlockSpec(memory_space=pltpu.VMEM)] * 2,
         scratch_shapes=[
             pltpu.VMEM(wall_mask.shape, jnp.int32),
             pltpu.VMEM(frac.shape, jnp.bfloat16),
@@ -601,10 +579,8 @@
             pltpu.VMEM(ends, f32),
             pltpu.VMEM((planes + 1, rows, half), f32),
             pltpu.VMEM((2, planes + 1, rows, half), f32),
-            pltpu.VMEM((planes + 1, rows, around), f32),
             dma,
             dma((8,)),
-            dma((planes + 3,)),
             dma((2,)),
             dma((planes,)),
             dma((planes,)),
@@ -632,25 +608,6 @@
         jnp.asarray(back),
         jnp.asarray(first.reshape(rows * rows, half)),
     )
-    chunk = planes // CORRECT_STEPS if planes % CORRECT_STEPS == 0 else planes
-    here = pl.BlockSpec((chunk, rows, around), lambda k: (k, 0, 0))
-    later = pl.BlockSpec((1, rows, around), lambda k: ((k + 1) * chunk, 0, 0))
-    return pl.pallas_call(
-        correct_kernel,
-        grid=(planes // chunk,),
-        out_shape=(
-            jax.ShapeDtypeStruct((planes, rows, around), f32),
-            jax.ShapeDtypeStruct((1, 3, planes, rows, around), jnp.bfloat16),
-        ),
-        in_specs=[
-            here,
-            later,
-            pl.BlockSpec((3, chunk, rows, around), lambda k: (0, k, 0, 0)),
-            here,
-            later,
-        ],
-        out_specs=(here, pl.BlockSpec((1, 3, chunk, rows, around), lambda k: (0, 0, k, 0, 0))),
-    )(space, space, pred, fluid, fluid)
 
 
 def solution(mesh):

time: 39 us -> 37.1 us (0.951)
  Pallas kernels: 37.5 us -> 34 us
  local copies, waits for them, and re-layouts: 0 us -> 1.67 us
    pallas_call x2 -> x1, Pallas kernels: 37.5 us -> 34 us  [drum_step(): pl.pallas_call(functools.partial(drum_kernel, gz_count), out_shape=(pltpu...]
    unnamed x0 -> x2, local copies, waits for them, and re-layouts: none -> 1.67 us
where the time goes in v1:
time: 37.1 us; the launch traced here: 36.9 us
  Pallas kernels  34 us (92%)
  local copies, waits for them, and re-layouts  1.67 us (5%)
  between operations  1.29 us (3%)
    pallas_call x1, Pallas kernels, drum_step(): pl.pallas_call(functools.partial(drum_kernel, gz_count), out_shape=(pltpu...  34 us
    unnamed x2, local copies, waits for them, and re-layouts  1.67 us

profile of v1, /device:TPU:0, one launch (start us, length us, event | category | flops | bytes accessed | tf_op | source)
XLA Modules:
  0.0 36.9 jit_solution(6440044284291075131)
XLA Ops:
  1.3 34.0 %shard_map.131 = (f32[8,64,256]{2,1,0:T(8,128)S(1)}, bf16[1,3,8,64,256]{4,3,2,1,0:T(8,128)(2,1)S(1)}) custom-call(s32[128]{0:T(128)} %offsets_ref.1, f32[32]{0:T(128)} %diameters_ref.1, s32[1]{0:T(128)S(6)} %copy.18.map_ref, s32[64,256]{1,0:T(8,128)} %wall_hbm.1, bf16[1,8,64,256]{3,2,1,0:T(8,128)(2,1)} %frac_hbm.1, bf16[1,3,8,64,256]{4,3,2,1,0:T(8,128)(2,1)} %velocity_hbm.1, ...), custom_call_target="tpu_custom_call" | custom-call | tf_op jit(solution)/shard_map/pallas_call | solution.py:549
  35.3 0.8 %copy.16 = f32[8,64,256]{2,1,0:T(8,128)} copy(f32[8,64,256]{2,1,0:T(8,128)S(1)} %get-tuple-element.2) | data formatting | bytes 1048576
  36.1 0.9 %copy.17 = bf16[1,3,8,64,256]{4,3,2,1,0:T(8,128)(2,1)} copy(bf16[1,3,8,64,256]{4,3,2,1,0:T(8,128)(2,1)S(1)} %get-tuple-element.3) | data formatting | bytes 1572864

commit v2 on v1

--- a/solution.py
+++ b/solution.py
@@ -186,8 +186,7 @@
     vectors = np.stack(vectors, -1)
     values = np.maximum(np.stack(values, -1), 0.0)
     first = vectors[:, :, :half]
-    nyquist = np.zeros((radial, max(radial, 128)))
-    nyquist[:, :radial] = vectors[:, :, half].T
+    last = vectors[:, :, half]
     other = np.concatenate([values[:, half:], values[:, 1:half]], -1)
     over = COMPRESS + np.stack([values[:, :half], other])
     root = np.sqrt(over * (over + 4.0))
@@ -196,18 +195,27 @@
     wrap = 1.0 / (1.0 - ratio**axial)
     line = np.stack([ratio, 1.0 / root, jump, wrap], 1).astype(np.float32)
     ahead = np_high_low(basis)
-    back = np_high_low(basis.T.copy())
+    back = np_high_low(basis.T.reshape(2, half, around))
+    nyquist = np_high_low(np.stack([last.T, last]))
     return (
         first.astype(np.float32),
-        nyquist.astype(np.float32),
+        np.stack(nyquist),
         line,
         np.stack(ahead),
         np.stack(back),
     )
 
 
+def left_triple(table_high, table_low, x):
+    high, low = split_low(x)
+    out = jnp.dot(table_high, high, preferred_element_type=jnp.float32)
+    out = out + jnp.dot(table_high, low, preferred_element_type=jnp.float32)
+    return out + jnp.dot(table_low, high, preferred_element_type=jnp.float32)
+
+
 def drum_kernel(
     gz_count,
+    group,
     offsets_ref,
     diameters_ref,
     map_ref,
@@ -230,6 +238,8 @@
     nyquist_ref,
     line_ref,
     back_ref,
+    radial,
+    radial_back,
     fluid,
     pred,
     term,
@@ -237,26 +247,22 @@
     halo,
     modes,
     partner,
-    radial,
-    radial_back,
     lines,
     ends_out,
     ends_in,
     states_out,
     states_in,
     solved,
-    result,
-    table_sem,
+    space,
     input_sem,
     halo_sem,
     swap_send,
     swap_recv,
-    ends_send,
-    ends_recv,
+    lines_sem,
+    ends_sem,
     states_send,
     states_recv,
-    back_send,
-    back_recv,
+    relay_sem,
 ):
     me = lax.axis_index("gz")
     ph = lax.axis_index("ph")
@@ -267,52 +273,45 @@
     blocks = rows // 8
     angle_step = 2.0 * math.pi / around
 
+    pairs = (
+        (wall_hbm, wall_ref),
+        (frac_hbm, frac_ref),
+        (velocity_hbm, velocity_ref),
+        (gas_hbm, gas_ref),
+        (ahead_hbm, ahead_ref),
+        (radial_hbm, radial),
+        (nyquist_hbm, nyquist_ref),
+        (line_hbm, line_ref),
+        (back_hbm, back_ref),
+    )
+    fetches = [pltpu.make_async_copy(a, b, input_sem.at[i]) for i, (a, b) in enumerate(pairs)]
+    for fetch in fetches[:4]:
+        fetch.start()
     barrier = pltpu.get_barrier_semaphore()
     for hop in range(1, gz_count):
         pl.semaphore_signal(
             barrier, inc=1, device_id=(lax.rem(me + hop, gz_count), ph), device_id_type=MESH_ID
         )
     pl.semaphore_signal(barrier, inc=1, device_id=(me, other), device_id_type=MESH_ID)
-
-    pairs = (
-        (wall_hbm, wall_ref),
-        (frac_hbm, frac_ref),
-        (velocity_hbm, velocity_ref),
-        (gas_hbm, gas_ref),
-        (ahead_hbm, ahead_ref),
-        (nyquist_hbm, nyquist_ref),
-        (line_hbm, line_ref),
-        (back_hbm, back_ref),
-    )
-    fetches = [pltpu.make_async_copy(a, b, input_sem.at[i]) for i, (a, b) in enumerate(pairs)]
-    table_copy = pltpu.make_async_copy(radial_hbm, radial, table_sem)
-    for fetch in fetches[:5]:
+    for fetch in fetches[4:]:
         fetch.start()
-    table_copy.start()
-    for fetch in fetches[5:]:
-        fetch.start()
-    fetches[0].wait()
 
     radii = lax.broadcasted_iota(jnp.int32, (rows, around), 0).astype(jnp.float32) + 0.5
     row_id = lax.broadcasted_iota(jnp.int32, (rows, around), 0)
-    wall = wall_ref[...].astype(jnp.float32).astype(jnp.bfloat16)
-    from_col = lax.broadcasted_iota(jnp.int32, (around, around), 0)
-    to_col = lax.broadcasted_iota(jnp.int32, (around, around), 1)
-    gap = to_col - from_col
+    lane = lax.broadcasted_iota(jnp.int32, (rows, half), 1)
+
+    fetches[0].wait()
+    wall = wall_ref[...].astype(jnp.float32)
 
     def rotate(z, carry):
         turn = offsets_ref[lax.rem(me * planes + z, axial_total)]
-        hit = (gap == turn) | (gap == turn - around)
-        one_hot = jnp.where(hit, 1.0, 0.0).astype(jnp.bfloat16)
-        fluid[z] = jnp.dot(wall, one_hot, preferred_element_type=jnp.float32)
+        fluid[z] = pltpu.roll(wall, turn, 1)
         return carry
 
     lax.fori_loop(0, planes + 1, rotate, 0)
-
     for fetch in fetches[1:4]:
         fetch.wait()
     size = diameters_ref[map_ref[0]]
-    axial_flux[0] = jnp.zeros((rows, around), jnp.float32)
 
     def opens(z):
         here = fluid[z]
@@ -323,7 +322,7 @@
     weight = -jnp.sqrt(radii) / DT_STEP
     share = 1.0 / lax.axis_size("ph")
 
-    def source(z, carry):
+    def source(z):
         volume = frac_ref[0, z].astype(jnp.float32)
         gas = [gas_ref[a, z].astype(jnp.float32) for a in range(3)]
         slip = [velocity_ref[0, a, z].astype(jnp.float32) - gas[a] for a in range(3)]
@@ -337,21 +336,34 @@
         flux_radial = (pull * slip[0] + share * gas[0]) * open_radial
         flux_around = (pull * slip[1] + share * gas[1]) * open_around
         flux_axial = (pull * slip[2] + share * gas[2]) * open_axial
-        axial_flux[z + 1] = flux_axial
         out = (radii + 0.5) * flux_radial
         inward = jnp.where(row_id == 0, 0.0, pltpu.roll(out, 1, 0))
         total = (out - inward) / radii
         total = total + (flux_around - pltpu.roll(flux_around, 1, 1)) / (radii * angle_step)
-        term[z] = (total + flux_axial - axial_flux[z]) * weight
-        return carry
-
-    lax.fori_loop(0, planes, source, 0)
-
+        term[z] = (total + flux_axial) * weight
+        return flux_axial
+
+    def swap(z):
+        return pltpu.make_async_remote_copy(
+            src_ref=modes.at[other, z],
+            dst_ref=partner.at[z],
+            send_sem=swap_send,
+            recv_sem=swap_recv.at[z],
+            device_id=(me, other),
+            device_id_type=MESH_ID,
+        )
+
+    def to_modes(z, behind):
+        out = triple_dot(term[z] - behind * weight, ahead_ref[0], ahead_ref[1])
+        modes[0, z] = out[:, :half]
+        modes[1, z] = out[:, half:]
+        swap(z).start()
+
+    axial_flux[...] = source(planes - 1)
     fetches[4].wait()
     pl.semaphore_wait(barrier, gz_count)
-
     halo_copy = pltpu.make_async_remote_copy(
-        src_ref=axial_flux.at[planes],
+        src_ref=axial_flux,
         dst_ref=halo,
         send_sem=halo_sem.at[0],
         recv_sem=halo_sem.at[1],
@@ -360,87 +372,116 @@
     )
     halo_copy.start()
 
-    def swap(z):
+    def send_modes(k, carry):
+        z = planes - 2 - k
+        to_modes(z + 1, source(z))
+        return carry
+
+    lax.fori_loop(0, planes - 1, send_modes, 0)
+    halo_copy.wait()
+    to_modes(0, halo[...])
+
+    for fetch in fetches[5:]:
+        fetch.wait()
+
+    def apply(table, loads):
+        def add(k, accs):
+            accs = list(accs)
+            for j in range(8):
+                r = k * 8 + j
+                part = table[pl.ds(pl.multiple_of(r * rows, rows), rows), :]
+                for i, load in enumerate(loads):
+                    accs[i] = accs[i] + part * jnp.broadcast_to(load(r), (rows, half))
+            return tuple(accs)
+
+        zero = jnp.zeros((rows, half), jnp.float32)
+        return lax.fori_loop(0, rows // 8, add, (zero,) * len(loads))
+
+    def patch(which, h, x, out):
+        exact = left_triple(nyquist_ref[0, which], nyquist_ref[1, which], x)
+        return jnp.where(lane + (1 - h) == 0, exact, out)
+
+    def share_lines(z, h):
         return pltpu.make_async_remote_copy(
-            src_ref=modes.at[other, z],
-            dst_ref=partner.at[z],
-            send_sem=swap_send.at[z],
-            recv_sem=swap_recv.at[z],
+            src_ref=lines.at[h, z],
+            dst_ref=lines.at[h, z],
+            send_sem=lines_sem.at[0],
+            recv_sem=lines_sem.at[1],
             device_id=(me, other),
             device_id_type=MESH_ID,
         )
 
-    def to_modes(z, value):
-        out = triple_dot(value, ahead_ref[0], ahead_ref[1])
-        modes[0, z] = out[:, :half]
-        modes[1, z] = out[:, half:]
-        swap(z).start()
-
-    def send_modes(k, carry):
-        to_modes(k, term[k])
+    def forward(k, carry):
+        z = planes - 1 - k
+        swap(z).wait_recv()
+        x = modes[ph, z] + partner[z]
+        partner[z] = x
+        (out,) = apply(radial, [lambda r: partner[z, pl.ds(r, 1), :]])
+        lines[ph, z] = patch(0, ph, x, out)
+        share_lines(z, ph).start()
         return carry
 
-    lax.fori_loop(1, planes, send_modes, 0)
-    halo_copy.wait()
-    to_modes(0, term[0] - halo[...] * weight)
-
-    table_copy.wait()
-    for fetch in fetches[5:]:
-        fetch.wait()
-    is_other = jnp.where(ph == 1, 1, 0)
-    lane0 = (lax.broadcasted_iota(jnp.int32, (rows, half), 1) == 0) & (
-        jnp.broadcast_to(is_other, (rows, half)) == 1
-    )
-    for r in range(rows):
-        fill = jnp.broadcast_to(nyquist_ref[:, r : r + 1], (rows, half))
-        radial[pl.ds(r * rows, rows), :] = jnp.where(lane0, fill, radial[pl.ds(r * rows, rows), :])
-
-    def apply(table, load, z):
-        def add(k, acc):
-            for j in range(8):
-                r = k * 8 + j
-                line = jnp.broadcast_to(load(z, r), (rows, half))
-                acc = acc + table[pl.ds(pl.multiple_of(r * rows, rows), rows), :] * line
-            return acc
-
-        return lax.fori_loop(0, rows // 8, add, jnp.zeros((rows, half), jnp.float32))
-
-    def load_term(z, r):
-        return modes[ph, z, pl.ds(r, 1), :] + partner[z, pl.ds(r, 1), :]
-
-    def forward(k, carry):
-        z = lax.rem(k + 1, planes)
-        swap(z).wait_recv()
-        lines[z] = apply(radial, load_term, z)
-        return carry
-
     lax.fori_loop(0, planes, forward, 0)
 
     ratio = line_ref[ph, 0]
-    rising = lines[0]
+    rising = lines[ph, 0]
     for z in range(1, planes):
-        rising = rising * ratio + lines[z]
-    falling = lines[planes - 1]
+        rising = rising * ratio + lines[ph, z]
+    falling = lines[ph, planes - 1]
     for z in range(planes - 2, -1, -1):
-        falling = falling * ratio + lines[z]
+        falling = falling * ratio + lines[ph, z]
     for j in range(blocks):
         ends_out[j] = rising[8 * j : 8 * j + 8]
         ends_out[blocks + j] = falling[8 * j : 8 * j + 8]
 
-    def exchange(src, dst, send, recv, hop, sender):
+    def give_ends(hop):
         to = lax.rem(me + hop, gz_count)
-        at = lax.rem(me + gz_count - hop, gz_count) if sender else me
         return pltpu.make_async_remote_copy(
-            src_ref=src.at[to],
-            dst_ref=dst.at[at],
-            send_sem=send.at[hop],
-            recv_sem=recv.at[hop],
+            src_ref=ends_out.at[to],
+            dst_ref=ends_in.at[me],
+            send_sem=ends_sem.at[0],
+            recv_sem=ends_sem.at[1],
             device_id=(to, ph),
             device_id_type=MESH_ID,
         )
 
+    def give_states(hop):
+        to = lax.rem(me + hop, gz_count)
+        return pltpu.make_async_remote_copy(
+            src_ref=states_out.at[to],
+            dst_ref=states_in.at[ph, me],
+            send_sem=states_send,
+            recv_sem=states_recv.at[hop],
+            device_id=(to, ph),
+            device_id_type=MESH_ID,
+        )
+
+    def relay(at, h):
+        return pltpu.make_async_remote_copy(
+            src_ref=states_in.at[h, at],
+            dst_ref=states_in.at[h, at],
+            send_sem=relay_sem.at[0],
+            recv_sem=relay_sem.at[1],
+            device_id=(me, other),
+            device_id_type=MESH_ID,
+        )
+
+    def whole(ref, send, recv):
+        return pltpu.make_async_remote_copy(
+            src_ref=ref,
+            dst_ref=ref,
+            send_sem=send,
+            recv_sem=recv,
+            device_id=(me, other),
+            device_id_type=MESH_ID,
+        )
+
+    sent_ends = whole(ends_in.at[pl.ds(0, gz_count - 1)], ends_sem.at[0], ends_sem.at[1])
+    sent_lines = whole(lines.at[other], lines_sem.at[0], lines_sem.at[1])
+    sent_relay = whole(states_in.at[other], relay_sem.at[0], relay_sem.at[1])
+
     for hop in range(1, gz_count):
-        exchange(ends_out, ends_in, ends_send, ends_recv, hop, False).start()
+        give_ends(hop).start()
     ends_in[me] = ends_out[me]
 
     def flip(l, carry):
@@ -450,9 +491,7 @@
         return carry
 
     lax.fori_loop(0, rows, flip, 0)
-
-    for hop in range(1, gz_count):
-        exchange(ends_out, ends_in, ends_send, ends_recv, hop, True).wait_recv()
+    sent_ends.wait_recv()
 
     is_rise = 1 - me // blocks
     mine = lax.rem(me, blocks)
@@ -468,74 +507,73 @@
         state = state * jump + ends_in[order[s]]
 
     for hop in range(1, gz_count):
-        exchange(states_out, states_in, states_send, states_recv, hop, False).start()
-    states_in[me] = states_out[me]
+        give_states(hop).start()
+    states_in[ph, me] = states_out[me]
+    relay(me, ph).start()
     for hop in range(1, gz_count):
-        exchange(states_out, states_in, states_send, states_recv, hop, True).wait_recv()
-
-    scale = line_ref[ph, 1]
-    right = jnp.concatenate([states_in[blocks + j] for j in range(blocks)], 0)
-    left = jnp.concatenate([states_in[j] for j in range(blocks)], 0)
-    solved[planes] = right
-    behind = right * ratio
-    for z in range(planes - 1, -1, -1):
-        solved[z] = behind
-        behind = (behind + lines[z]) * ratio
-    ahead_state = left
-    for z in range(planes):
-        ahead_state = ahead_state * ratio + lines[z]
-        solved[z] = (solved[z] + ahead_state) * scale
-    solved[planes] = (solved[planes] + ahead_state * ratio) * scale
-
-    def give(z, index):
-        return pltpu.make_async_remote_copy(
-            src_ref=result.at[index, z],
-            dst_ref=result.at[index, z],
-            send_sem=back_send.at[z],
-            recv_sem=back_recv.at[z],
-            device_id=(me, other),
-            device_id_type=MESH_ID,
-        )
-
-    def load_solved(z, r):
-        return solved[z, pl.ds(r, 1), :]
+        give_states(hop).wait_recv()
+        relay(lax.rem(me + gz_count - hop, gz_count), ph).start()
+
+    def solve(h):
+        ratio = line_ref[h, 0]
+        scale = line_ref[h, 1]
+        right = jnp.concatenate([states_in[h, blocks + j] for j in range(blocks)], 0)
+        left = jnp.concatenate([states_in[h, j] for j in range(blocks)], 0)
+        last = right
+        behind = right * ratio
+        for z in range(planes - 1, -1, -1):
+            solved[z] = behind
+            behind = (behind + lines[h, z]) * ratio
+        for z in range(planes):
+            left = left * ratio + lines[h, z]
+            solved[z] = (solved[z] + left) * scale
+        solved[planes] = (last + left * ratio) * scale
 
     shrink = 1.0 / jnp.sqrt(radii[:, :half])
 
-    def inverse(z, carry):
-        result[ph, z] = apply(radial_back, load_solved, z) * shrink
-        give(z, ph).start()
+    def inverse(h, k):
+        at = [k * group + i for i in range(group)]
+        outs = apply(radial_back, [lambda r, z=z: solved[z, pl.ds(r, 1), :] for z in at])
+        outs = [patch(1, h, solved[z], out) * shrink for z, out in zip(at, outs)]
+        whole_rows = jnp.concatenate(outs, 0)
+        found = triple_dot(whole_rows, back_ref[0, h], back_ref[1, h])
+        return [found[i * rows : (i + 1) * rows] for i in range(group)]
+
+    solve(ph)
+
+    def own_half(k, carry):
+        for i, part in enumerate(inverse(ph, k)):
+            space[k * group + i] = part
         return carry
 
-    lax.fori_loop(0, planes + 1, inverse, 0)
-
+    lax.fori_loop(0, (planes + 1) // group, own_half, 0)
+
+    sent_lines.wait_recv()
+    sent_relay.wait_recv()
+    solve(other)
     arc = 1.0 / (radii * angle_step)
 
-    def finish(z):
-        give(z, other).wait_recv()
-        both = jnp.concatenate([result[0, z], result[1, z]], 1)
-        return triple_dot(both, back_ref[0], back_ref[1])
-
-    def correct(z, here):
-        later = finish(z + 1)
+    def correct(z):
+        here = space[z]
         pressure_ref[z] = here
         open_radial, open_around, open_axial = opens(z)
         radial_step = (pltpu.roll(here, rows - 1, 0) - here) * open_radial
         around_step = (pltpu.roll(here, around - 1, 1) - here) * arc * open_around
-        axial_step = (later - here) * open_axial
+        axial_step = (space[z + 1] - here) * open_axial
         for a, step in enumerate((radial_step, around_step, axial_step)):
             corrected_ref[0, a, z] = (pred[a, z] - DT_STEP * step).astype(jnp.bfloat16)
-        return later
-
-    lax.fori_loop(0, planes, correct, finish(0))
-
-    for z in range(planes):
-        swap(z).wait_send()
-    for hop in range(1, gz_count):
-        exchange(ends_out, ends_in, ends_send, ends_recv, hop, False).wait_send()
-        exchange(states_out, states_in, states_send, states_recv, hop, False).wait_send()
-    for z in range(planes + 1):
-        give(z, ph).wait_send()
+
+    for k in range((planes + 1) // group):
+        for i, part in enumerate(inverse(other, k)):
+            space[k * group + i] = space[k * group + i] + part
+        for z in range(max(k * group - 1, 0), (k + 1) * group - 1):
+            correct(z)
+
+    whole(modes.at[other], swap_send, swap_recv.at[0]).wait_send()
+    sent_lines.wait_send()
+    sent_ends.wait_send()
+    whole(states_out.at[pl.ds(0, gz_count - 1)], states_send, states_recv.at[0]).wait_send()
+    sent_relay.wait_send()
 
 
 def drum_step(gz_count, frac, velocity, gas_vel, diameters, phase_map, wall_mask, offsets):
@@ -546,8 +584,9 @@
     f32 = jnp.float32
     dma = pltpu.SemaphoreType.DMA
     ends = (gz_count, 8, half)
+    group = 3 if (planes + 1) % 3 == 0 else 1
     return pl.pallas_call(
-        functools.partial(drum_kernel, gz_count),
+        functools.partial(drum_kernel, gz_count, group),
         out_shape=(
             pltpu.VMEM((planes, rows, around), f32),
             pltpu.VMEM((1, 3, planes, rows, around), jnp.bfloat16),
@@ -560,36 +599,34 @@
             pltpu.VMEM(velocity.shape, jnp.bfloat16),
             pltpu.VMEM(gas_vel.shape, jnp.bfloat16),
             pltpu.VMEM(ahead.shape, jnp.bfloat16),
-            pltpu.VMEM(nyquist.shape, f32),
+            pltpu.VMEM(nyquist.shape, jnp.bfloat16),
             pltpu.VMEM(line.shape, f32),
             pltpu.VMEM(back.shape, jnp.bfloat16),
+            pltpu.VMEM((rows * rows, half), f32),
+            pltpu.VMEM((rows * rows, half), f32),
             pltpu.VMEM((planes + 1, rows, around), f32),
             pltpu.VMEM((3, planes, rows, around), f32),
             pltpu.VMEM((planes, rows, around), f32),
-            pltpu.VMEM((planes + 1, rows, around), f32),
+            pltpu.VMEM((rows, around), f32),
             pltpu.VMEM((rows, around), f32),
             pltpu.VMEM((2, planes, rows, half), f32),
             pltpu.VMEM((planes, rows, half), f32),
-            pltpu.VMEM((rows * rows, half), f32),
-            pltpu.VMEM((rows * rows, half), f32),
-            pltpu.VMEM((planes, rows, half), f32),
+            pltpu.VMEM((2, planes, rows, half), f32),
             pltpu.VMEM(ends, f32),
             pltpu.VMEM(ends, f32),
             pltpu.VMEM(ends, f32),
-            pltpu.VMEM(ends, f32),
+            pltpu.VMEM((2, *ends), f32),
             pltpu.VMEM((planes + 1, rows, half), f32),
-            pltpu.VMEM((2, planes + 1, rows, half), f32),
+            pltpu.VMEM((planes + 1, rows, around), f32),
+            dma((9,)),
+            dma((2,)),
             dma,
-            dma((8,)),
+            dma((planes,)),
             dma((2,)),
-            dma((planes,)),
-            dma((planes,)),
+            dma((2,)),
+            dma,
             dma((gz_count,)),
-            dma((gz_count,)),
-            dma((gz_count,)),
-            dma((gz_count,)),
-            dma((planes + 1,)),
-            dma((planes + 1,)),
+            dma((2,)),
         ],
         compiler_params=pltpu.CompilerParams(
             collective_id=0, has_side_effects=True, vmem_limit_bytes=56 * 1024 * 1024

time: 37.1 us -> 33.8 us (0.911)
  Pallas kernels: 34 us -> 30.7 us
    pallas_call x1, Pallas kernels: 34 us -> 30.7 us  [drum_step(): pl.pallas_call(functools.partial(drum_kernel, gz_count, group), out_shape...]
where the time goes in v2:
time: 33.8 us; the launch traced here: 33.6 us
  Pallas kernels  30.7 us (91%)
  local copies, waits for them, and re-layouts  1.67 us (5%)
  between operations  1.29 us (4%)
    pallas_call x1, Pallas kernels, drum_step(): pl.pallas_call(functools.partial(drum_kernel, gz_count, group), out_shape...  30.7 us
    unnamed x2, local copies, waits for them, and re-layouts  1.67 us

profile of v2, /device:TPU:0, one launch (start us, length us, event | category | flops | bytes accessed | tf_op | source)
XLA Modules:
  0.0 33.6 jit_solution(5654814148518312795)
XLA Ops:
  1.3 30.7 %shard_map.131 = (f32[8,64,256]{2,1,0:T(8,128)S(1)}, bf16[1,3,8,64,256]{4,3,2,1,0:T(8,128)(2,1)S(1)}) custom-call(s32[128]{0:T(128)} %offsets_ref.1, f32[32]{0:T(128)} %diameters_ref.1, s32[1]{0:T(128)S(6)} %copy.18.map_ref, s32[64,256]{1,0:T(8,128)} %wall_hbm.1, bf16[1,8,64,256]{3,2,1,0:T(8,128)(2,1)} %frac_hbm.1, bf16[1,3,8,64,256]{4,3,2,1,0:T(8,128)(2,1)} %velocity_hbm.1, ...), custom_call_target="tpu_custom_call" | custom-call | tf_op jit(solution)/shard_map/pallas_call | solution.py:588
  32.0 0.8 %copy.16 = f32[8,64,256]{2,1,0:T(8,128)} copy(f32[8,64,256]{2,1,0:T(8,128)S(1)} %get-tuple-element.2) | data formatting | bytes 1048576
  32.8 0.9 %copy.17 = bf16[1,3,8,64,256]{4,3,2,1,0:T(8,128)(2,1)} copy(bf16[1,3,8,64,256]{4,3,2,1,0:T(8,128)(2,1)S(1)} %get-tuple-element.3) | data formatting | bytes 1572864

commit v3 on v2

--- a/solution.py
+++ b/solution.py
@@ -196,10 +196,13 @@
     line = np.stack([ratio, 1.0 / root, jump, wrap], 1).astype(np.float32)
     ahead = np_high_low(basis)
     back = np_high_low(basis.T.reshape(2, half, around))
-    nyquist = np_high_low(np.stack([last.T, last]))
+    nyquist = np_high_low(last.T)
+    fill = np.zeros((radial, max(radial, 128)))
+    fill[:, :radial] = last / np.sqrt(radius)[:, None]
     return (
         first.astype(np.float32),
         np.stack(nyquist),
+        fill.astype(np.float32),
         line,
         np.stack(ahead),
         np.stack(back),
@@ -225,6 +228,7 @@
     gas_hbm,
     ahead_hbm,
     nyquist_hbm,
+    fill_hbm,
     line_hbm,
     back_hbm,
     radial_hbm,
@@ -236,12 +240,14 @@
     gas_ref,
     ahead_ref,
     nyquist_ref,
+    fill_ref,
     line_ref,
     back_ref,
     radial,
     radial_back,
     fluid,
     pred,
+    gates,
     term,
     axial_flux,
     halo,
@@ -253,6 +259,7 @@
     states_out,
     states_in,
     solved,
+    result,
     space,
     input_sem,
     halo_sem,
@@ -270,7 +277,10 @@
     planes, rows, around = term.shape
     half = around // 2
     axial_total = offsets_ref.shape[0]
-    blocks = rows // 8
+    owners = gz_count // 2
+    base = gz_count // 4
+    width = ends_in.shape[1]
+    blocks = owners // 2
     angle_step = 2.0 * math.pi / around
 
     pairs = (
@@ -281,6 +291,7 @@
         (ahead_hbm, ahead_ref),
         (radial_hbm, radial),
         (nyquist_hbm, nyquist_ref),
+        (fill_hbm, fill_ref),
         (line_hbm, line_ref),
         (back_hbm, back_ref),
     )
@@ -301,19 +312,20 @@
     lane = lax.broadcasted_iota(jnp.int32, (rows, half), 1)
 
     fetches[0].wait()
-    wall = wall_ref[...].astype(jnp.float32)
-
-    def rotate(z, carry):
+
+    def rotate(z):
         turn = offsets_ref[lax.rem(me * planes + z, axial_total)]
-        fluid[z] = pltpu.roll(wall, turn, 1)
-        return carry
-
-    lax.fori_loop(0, planes + 1, rotate, 0)
+        fluid[z] = pltpu.roll(wall_ref[...].astype(jnp.float32), turn, 1)
+
+    rotate(planes)
     for fetch in fetches[1:4]:
         fetch.wait()
     size = diameters_ref[map_ref[0]]
 
+    arc = 1.0 / (radii * angle_step)
+
     def opens(z):
+        rotate(z)
         here = fluid[z]
         open_radial = jnp.where(row_id == rows - 1, 0.0, here * pltpu.roll(here, rows - 1, 0))
         open_around = here * pltpu.roll(here, around - 1, 1)
@@ -332,6 +344,9 @@
         open_radial, open_around, open_axial = opens(z)
         for a in range(3):
             pred[a, z] = gas[a] + relax * slip[a]
+        gates[0, z] = DT_STEP * open_radial
+        gates[1, z] = (DT_STEP * arc) * open_around
+        gates[2, z] = DT_STEP * open_axial
         pull = volume * relax
         flux_radial = (pull * slip[0] + share * gas[0]) * open_radial
         flux_around = (pull * slip[1] + share * gas[1]) * open_around
@@ -339,7 +354,7 @@
         out = (radii + 0.5) * flux_radial
         inward = jnp.where(row_id == 0, 0.0, pltpu.roll(out, 1, 0))
         total = (out - inward) / radii
-        total = total + (flux_around - pltpu.roll(flux_around, 1, 1)) / (radii * angle_step)
+        total = total + (flux_around - pltpu.roll(flux_around, 1, 1)) * arc
         term[z] = (total + flux_axial) * weight
         return flux_axial
 
@@ -397,28 +412,14 @@
         zero = jnp.zeros((rows, half), jnp.float32)
         return lax.fori_loop(0, rows // 8, add, (zero,) * len(loads))
 
-    def patch(which, h, x, out):
-        exact = left_triple(nyquist_ref[0, which], nyquist_ref[1, which], x)
-        return jnp.where(lane + (1 - h) == 0, exact, out)
-
-    def share_lines(z, h):
-        return pltpu.make_async_remote_copy(
-            src_ref=lines.at[h, z],
-            dst_ref=lines.at[h, z],
-            send_sem=lines_sem.at[0],
-            recv_sem=lines_sem.at[1],
-            device_id=(me, other),
-            device_id_type=MESH_ID,
-        )
-
     def forward(k, carry):
         z = planes - 1 - k
         swap(z).wait_recv()
         x = modes[ph, z] + partner[z]
         partner[z] = x
         (out,) = apply(radial, [lambda r: partner[z, pl.ds(r, 1), :]])
-        lines[ph, z] = patch(0, ph, x, out)
-        share_lines(z, ph).start()
+        exact = left_triple(nyquist_ref[0], nyquist_ref[1], x)
+        lines[ph, z] = jnp.where(lane + other == 0, exact, out)
         return carry
 
     lax.fori_loop(0, planes, forward, 0)
@@ -431,27 +432,27 @@
     for z in range(planes - 2, -1, -1):
         falling = falling * ratio + lines[ph, z]
     for j in range(blocks):
-        ends_out[j] = rising[8 * j : 8 * j + 8]
-        ends_out[blocks + j] = falling[8 * j : 8 * j + 8]
-
-    def give_ends(hop):
-        to = lax.rem(me + hop, gz_count)
+        ends_out[j] = rising[width * j : width * j + width]
+        ends_out[blocks + j] = falling[width * j : width * j + width]
+
+    is_owner = (me >= base) & (me < base + owners)
+
+    def give_ends(o):
         return pltpu.make_async_remote_copy(
-            src_ref=ends_out.at[to],
+            src_ref=ends_out.at[o],
             dst_ref=ends_in.at[me],
             send_sem=ends_sem.at[0],
             recv_sem=ends_sem.at[1],
-            device_id=(to, ph),
+            device_id=(base + o, ph),
             device_id_type=MESH_ID,
         )
 
-    def give_states(hop):
-        to = lax.rem(me + hop, gz_count)
+    def give_states(to, o):
         return pltpu.make_async_remote_copy(
             src_ref=states_out.at[to],
-            dst_ref=states_in.at[ph, me],
+            dst_ref=states_in.at[ph, o],
             send_sem=states_send,
-            recv_sem=states_recv.at[hop],
+            recv_sem=states_recv.at[o],
             device_id=(to, ph),
             device_id_type=MESH_ID,
         )
@@ -477,42 +478,65 @@
         )
 
     sent_ends = whole(ends_in.at[pl.ds(0, gz_count - 1)], ends_sem.at[0], ends_sem.at[1])
-    sent_lines = whole(lines.at[other], lines_sem.at[0], lines_sem.at[1])
     sent_relay = whole(states_in.at[other], relay_sem.at[0], relay_sem.at[1])
-
-    for hop in range(1, gz_count):
-        give_ends(hop).start()
-    ends_in[me] = ends_out[me]
+    late = me // (gz_count // 2)
+
+    for k in range(owners):
+        o = lax.rem(k + (1 - late) * blocks, owners)
+
+        @pl.when(base + o != me)
+        def _(o=o):
+            give_ends(o).start()
+
+    share_lines = whole(lines.at[ph], lines_sem.at[0], lines_sem.at[1])
+    share_lines.start()
+
+    @pl.when(is_owner)
+    def _():
+        ends_in[me] = ends_out[me - base]
+
+    shrink = 1.0 / jnp.sqrt(radii[:, :half])
 
     def flip(l, carry):
-        radial_back[pl.ds(pl.multiple_of(l * rows, rows), rows), :] = radial[
-            pl.ds(l, rows, stride=rows), :
-        ]
+        at = pl.ds(pl.multiple_of(l * rows, rows), rows)
+        radial_back[0, at, :] = radial[pl.ds(l, rows, stride=rows), :] * shrink
         return carry
 
     lax.fori_loop(0, rows, flip, 0)
-    sent_ends.wait_recv()
-
-    is_rise = 1 - me // blocks
-    mine = lax.rem(me, blocks)
-    jump = line_ref[ph, 2, pl.ds(pl.multiple_of(mine * 8, 8), 8), :]
-    wrap = line_ref[ph, 3, pl.ds(pl.multiple_of(mine * 8, 8), 8), :]
-    order = [is_rise * s + (1 - is_rise) * (gz_count - 1 - s) for s in range(gz_count)]
-    state = jnp.zeros((8, half), jnp.float32)
-    for s in range(gz_count):
-        state = state * jump + ends_in[order[s]]
-    state = state * wrap
-    for s in range(gz_count):
-        states_out[order[s]] = state
-        state = state * jump + ends_in[order[s]]
-
-    for hop in range(1, gz_count):
-        give_states(hop).start()
-    states_in[ph, me] = states_out[me]
-    relay(me, ph).start()
-    for hop in range(1, gz_count):
-        give_states(hop).wait_recv()
-        relay(lax.rem(me + gz_count - hop, gz_count), ph).start()
+
+    @pl.when(is_owner)
+    def _():
+        sent_ends.wait_recv()
+        mine = me - base
+        is_rise = 1 - mine // blocks
+        at = pl.ds(pl.multiple_of(lax.rem(mine, blocks) * width, width), width)
+        jump = line_ref[ph, 2, at, :]
+        wrap = line_ref[ph, 3, at, :]
+        order = [is_rise * s + (1 - is_rise) * (gz_count - 1 - s) for s in range(gz_count)]
+        state = jnp.zeros((width, half), jnp.float32)
+        for s in range(gz_count):
+            state = state * jump + ends_in[order[s]]
+        state = state * wrap
+        for s in range(gz_count):
+            states_out[order[s]] = state
+            state = state * jump + ends_in[order[s]]
+        for hop in sorted(range(1, gz_count), key=lambda hop: abs(hop - gz_count // 2)):
+            give_states(lax.rem(me + hop, gz_count), mine).start()
+        states_in[ph, mine] = states_out[me]
+
+    for l in range(rows):
+        at = pl.ds(l * rows, rows)
+        fill = jnp.broadcast_to(fill_ref[:, l : l + 1], (rows, half))
+        radial_back[1, at, :] = jnp.where(lane == 0, fill, radial_back[0, at, :])
+
+    for k in range(owners):
+        o = lax.rem(k + late * blocks, owners)
+
+        @pl.when(base + o != me)
+        def _(o=o):
+            give_states(me, o).wait_recv()
+
+        relay(o, ph).start()
 
     def solve(h):
         ratio = line_ref[h, 0]
@@ -529,69 +553,88 @@
             solved[z] = (solved[z] + left) * scale
         solved[planes] = (last + left * ratio) * scale
 
-    shrink = 1.0 / jnp.sqrt(radii[:, :half])
+    groups = (planes + 1) // group
 
     def inverse(h, k):
-        at = [k * group + i for i in range(group)]
-        outs = apply(radial_back, [lambda r, z=z: solved[z, pl.ds(r, 1), :] for z in at])
-        outs = [patch(1, h, solved[z], out) * shrink for z, out in zip(at, outs)]
-        whole_rows = jnp.concatenate(outs, 0)
-        found = triple_dot(whole_rows, back_ref[0, h], back_ref[1, h])
-        return [found[i * rows : (i + 1) * rows] for i in range(group)]
+        loads = [lambda r, z=k * group + i: solved[z, pl.ds(r, 1), :] for i in range(group)]
+        return apply(radial_back.at[h], loads)
 
     solve(ph)
 
     def own_half(k, carry):
-        for i, part in enumerate(inverse(ph, k)):
-            space[k * group + i] = part
+        for i, out in enumerate(inverse(ph, k)):
+            result[k * group + i] = out
         return carry
 
-    lax.fori_loop(0, (planes + 1) // group, own_half, 0)
-
-    sent_lines.wait_recv()
+    lax.fori_loop(0, groups, own_half, 0)
+
+    share_lines.wait_recv()
     sent_relay.wait_recv()
     solve(other)
-    arc = 1.0 / (radii * angle_step)
 
     def correct(z):
         here = space[z]
         pressure_ref[z] = here
-        open_radial, open_around, open_axial = opens(z)
-        radial_step = (pltpu.roll(here, rows - 1, 0) - here) * open_radial
-        around_step = (pltpu.roll(here, around - 1, 1) - here) * arc * open_around
-        axial_step = (space[z + 1] - here) * open_axial
+        radial_step = (pltpu.roll(here, rows - 1, 0) - here) * gates[0, z]
+        around_step = (pltpu.roll(here, around - 1, 1) - here) * gates[1, z]
+        axial_step = (space[z + 1] - here) * gates[2, z]
         for a, step in enumerate((radial_step, around_step, axial_step)):
-            corrected_ref[0, a, z] = (pred[a, z] - DT_STEP * step).astype(jnp.bfloat16)
-
-    for k in range((planes + 1) // group):
-        for i, part in enumerate(inverse(other, k)):
-            space[k * group + i] = space[k * group + i] + part
-        for z in range(max(k * group - 1, 0), (k + 1) * group - 1):
+            corrected_ref[0, a, z] = (pred[a, z] - step).astype(jnp.bfloat16)
+
+    for k in range(groups):
+        outs = inverse(other, k)
+        own = jnp.concatenate([result[k * group + i] for i in range(group)], 0)
+        both = jnp.concatenate([own, jnp.concatenate(outs, 0)], 1)
+        table = [jnp.concatenate([back_ref[i, ph], back_ref[i, other]], 0) for i in range(2)]
+        found = triple_dot(both, *table)
+        for z in range(max((k - 1) * group - 1, 0), k * group - 1):
             correct(z)
+        for i in range(group):
+            space[k * group + i] = found[i * rows : (i + 1) * rows]
+    for z in range(max((groups - 1) * group - 1, 0), planes):
+        correct(z)
 
     whole(modes.at[other], swap_send, swap_recv.at[0]).wait_send()
-    sent_lines.wait_send()
-    sent_ends.wait_send()
-    whole(states_out.at[pl.ds(0, gz_count - 1)], states_send, states_recv.at[0]).wait_send()
+    share_lines.wait_send()
     sent_relay.wait_send()
+
+    @pl.when(is_owner)
+    def _():
+        whole(ends_out.at[pl.ds(0, owners - 1)], ends_sem.at[0], ends_sem.at[1]).wait_send()
+        sent = states_out.at[pl.ds(0, gz_count - 1)]
+        whole(sent, states_send, states_recv.at[0]).wait_send()
+
+    @pl.when(jnp.logical_not(is_owner))
+    def _():
+        whole(ends_out, ends_sem.at[0], ends_sem.at[1]).wait_send()
+
+
+def put_kernel(pressure_vmem, corrected_vmem, pressure_out, corrected_out, sem):
+    pairs = ((pressure_vmem, pressure_out), (corrected_vmem, corrected_out))
+    copies = [pltpu.make_async_copy(a, b, sem.at[i]) for i, (a, b) in enumerate(pairs)]
+    for copy in copies:
+        copy.start()
+    for copy in copies:
+        copy.wait()
 
 
 def drum_step(gz_count, frac, velocity, gas_vel, diameters, phase_map, wall_mask, offsets):
     planes, rows, around = frac.shape[1:]
     half = around // 2
-    first, nyquist, line, ahead, back = operator_tables(rows, around, offsets.shape[0], planes)
+    first, nyquist, fill, line, ahead, back = operator_tables(rows, around, offsets.shape[0], planes)
     smem = pl.BlockSpec(memory_space=pltpu.SMEM)
     f32 = jnp.float32
     dma = pltpu.SemaphoreType.DMA
-    ends = (gz_count, 8, half)
+    owners = gz_count // 2
+    width = 2 * rows // owners
     group = 3 if (planes + 1) % 3 == 0 else 1
-    return pl.pallas_call(
+    results = pl.pallas_call(
         functools.partial(drum_kernel, gz_count, group),
         out_shape=(
             pltpu.VMEM((planes, rows, around), f32),
             pltpu.VMEM((1, 3, planes, rows, around), jnp.bfloat16),
         ),
-        in_specs=[smem] * 3 + [pl.BlockSpec(memory_space=pl.ANY)] * 9,
+        in_specs=[smem] * 3 + [pl.BlockSpec(memory_space=pl.ANY)] * 10,
         out_specs=[pl.BlockSpec(memory_space=pltpu.VMEM)] * 2,
         scratch_shapes=[
             pltpu.VMEM(wall_mask.shape, jnp.int32),
@@ -600,11 +643,13 @@
             pltpu.VMEM(gas_vel.shape, jnp.bfloat16),
             pltpu.VMEM(ahead.shape, jnp.bfloat16),
             pltpu.VMEM(nyquist.shape, jnp.bfloat16),
+            pltpu.VMEM(fill.shape, f32),
             pltpu.VMEM(line.shape, f32),
             pltpu.VMEM(back.shape, jnp.bfloat16),
             pltpu.VMEM((rows * rows, half), f32),
-            pltpu.VMEM((rows * rows, half), f32),
+            pltpu.VMEM((2, rows * rows, half), f32),
             pltpu.VMEM((planes + 1, rows, around), f32),
+            pltpu.VMEM((3, planes, rows, around), f32),
             pltpu.VMEM((3, planes, rows, around), f32),
             pltpu.VMEM((planes, rows, around), f32),
             pltpu.VMEM((rows, around), f32),
@@ -612,20 +657,21 @@
             pltpu.VMEM((2, planes, rows, half), f32),
             pltpu.VMEM((planes, rows, half), f32),
             pltpu.VMEM((2, planes, rows, half), f32),
-            pltpu.VMEM(ends, f32),
-            pltpu.VMEM(ends, f32),
-            pltpu.VMEM(ends, f32),
-            pltpu.VMEM((2, *ends), f32),
+            pltpu.VMEM((owners, width, half), f32),
+            pltpu.VMEM((gz_count, width, half), f32),
+            pltpu.VMEM((gz_count, width, half), f32),
+            pltpu.VMEM((2, owners, width, half), f32),
+            pltpu.VMEM((planes + 1, rows, half), f32),
             pltpu.VMEM((planes + 1, rows, half), f32),
             pltpu.VMEM((planes + 1, rows, around), f32),
-            dma((9,)),
+            dma((10,)),
             dma((2,)),
             dma,
             dma((planes,)),
             dma((2,)),
             dma((2,)),
             dma,
-            dma((gz_count,)),
+            dma((owners,)),
             dma((2,)),
         ],
         compiler_params=pltpu.CompilerParams(
@@ -641,10 +687,19 @@
         gas_vel,
         jnp.asarray(ahead),
         jnp.asarray(nyquist),
+        jnp.asarray(fill),
         jnp.asarray(line),
         jnp.asarray(back),
         jnp.asarray(first.reshape(rows * rows, half)),
     )
+    return pl.pallas_call(
+        put_kernel,
+        out_shape=tuple(jax.ShapeDtypeStruct(x.shape, x.dtype) for x in results),
+        in_specs=[pl.BlockSpec(memory_space=pltpu.VMEM)] * 2,
+        out_specs=[pl.BlockSpec(memory_space=pl.ANY)] * 2,
+        scratch_shapes=[dma((2,))],
+        compiler_params=pltpu.CompilerParams(vmem_limit_bytes=4 * 1024 * 1024),
+    )(*(pltpu.with_memory_space_constraint(x, pltpu.VMEM) for x in results))
 
 
 def solution(mesh):
@@ -662,7 +717,7 @@
 
     def body(frac, *rest):
         rows, around = frac.shape[2:]
-        fits = ph_count == 2 and around == 256 and rows <= 128
+        fits = ph_count == 2 and around == 256 and rows <= 128 and gz_count % 4 == 0
         if fits and rows * 2 == gz_count * 8 and frac.shape[1] <= 8:
             return drum_step(gz_count, frac, *rest)
         return shards(frac, *rest)

time: 33.8 us -> 31 us (0.917)
  local copies, waits for them, and re-layouts: 1.67 us -> 0 us
  Pallas kernels: 30.7 us -> 29.5 us
    pallas_call x1, Pallas kernels: 30.7 us -> 28.4 us  [drum_step(): pl.pallas_call(functools.partial(drum_kernel, gz_count, group), out_shape...]
    unnamed x2 -> x0, local copies, waits for them, and re-layouts: 1.67 us -> none
    pallas_call x0 -> x1, Pallas kernels: none -> 1.07 us  [drum_step(): pl.pallas_call(put_kernel, out_shape=tuple((jax.ShapeDtypeStruct(x.shape,...]
where the time goes in v3:
time: 31 us; the launch traced here: 30.8 us
  Pallas kernels  29.5 us (95%)
  between operations  1.29 us (4%)
    pallas_call x1, Pallas kernels, drum_step(): pl.pallas_call(functools.partial(drum_kernel, gz_count, group), out_shape...  28.4 us
    pallas_call x1, Pallas kernels, drum_step(): pl.pallas_call(put_kernel, out_shape=tuple((jax.ShapeDtypeStruct(x.shape,...  1.07 us

profile of v3, /device:TPU:0, one launch (start us, length us, event | category | flops | bytes accessed | tf_op | source)
XLA Modules:
  0.0 30.8 jit_solution(3131721252542077472)
XLA Ops:
  1.3 28.4 %shard_map.140 = (f32[8,64,256]{2,1,0:T(8,128)S(1)}, bf16[1,3,8,64,256]{4,3,2,1,0:T(8,128)(2,1)S(1)}) custom-call(s32[128]{0:T(128)} %offsets_ref.1, f32[32]{0:T(128)} %diameters_ref.1, s32[1]{0:T(128)S(6)} %copy.15.map_ref, s32[64,256]{1,0:T(8,128)} %wall_hbm.1, bf16[1,8,64,256]{3,2,1,0:T(8,128)(2,1)} %frac_hbm.1, bf16[1,3,8,64,256]{4,3,2,1,0:T(8,128)(2,1)} %velocity_hbm.1, ...), custom_call_target="tpu_custom_call" | custom-call | tf_op jit(solution)/shard_map/pallas_call | solution.py:631
  29.7 1.1 %shard_map.141 = (f32[8,64,256]{2,1,0:T(8,128)}, bf16[1,3,8,64,256]{4,3,2,1,0:T(8,128)(2,1)}) custom-call(f32[8,64,256]{2,1,0:T(8,128)S(1)} %get-tuple-element.4.pressure_vmem, bf16[1,3,8,64,256]{4,3,2,1,0:T(8,128)(2,1)S(1)} %get-tuple-element.5.corrected_vmem), custom_call_target="tpu_custom_call" | custom-call | tf_op jit(solution)/shard_map/pallas_call | solution.py:695

commit v4 on v3

--- a/solution.py
+++ b/solution.py
@@ -218,7 +218,6 @@
 
 def drum_kernel(
     gz_count,
-    group,
     offsets_ref,
     diameters_ref,
     map_ref,
@@ -270,6 +269,7 @@
     states_send,
     states_recv,
     relay_sem,
+    known_sem,
 ):
     me = lax.axis_index("gz")
     ph = lax.axis_index("ph")
@@ -283,11 +283,14 @@
     blocks = owners // 2
     angle_step = 2.0 * math.pi / around
 
-    pairs = (
-        (wall_hbm, wall_ref),
-        (frac_hbm, frac_ref),
-        (velocity_hbm, velocity_ref),
-        (gas_hbm, gas_ref),
+    last = planes - 1
+    streams = ((frac_hbm, frac_ref), (velocity_hbm, velocity_ref), (gas_hbm, gas_ref))
+
+    def part(ref, start, count):
+        lead = (slice(None),) * (len(ref.shape) - 3)
+        return ref.at[(*lead, pl.ds(start, count))]
+
+    tables = (
         (ahead_hbm, ahead_ref),
         (radial_hbm, radial),
         (nyquist_hbm, nyquist_ref),
@@ -295,31 +298,48 @@
         (line_hbm, line_ref),
         (back_hbm, back_ref),
     )
+    pairs = [(part(a, last, 1), part(b, last, 1)) for a, b in streams]
+    pairs += [(wall_hbm, wall_ref)]
+    pairs += [(part(a, 0, last), part(b, 0, last)) for a, b in streams]
+    pairs += tables
     fetches = [pltpu.make_async_copy(a, b, input_sem.at[i]) for i, (a, b) in enumerate(pairs)]
+    barrier = pltpu.get_barrier_semaphore()
     for fetch in fetches[:4]:
         fetch.start()
-    barrier = pltpu.get_barrier_semaphore()
-    for hop in range(1, gz_count):
-        pl.semaphore_signal(
-            barrier, inc=1, device_id=(lax.rem(me + hop, gz_count), ph), device_id_type=MESH_ID
-        )
+    for to in ((lax.rem(me + 1, gz_count), ph), (lax.rem(me + gz_count - 1, gz_count), ph)):
+        pl.semaphore_signal(barrier, inc=1, device_id=to, device_id_type=MESH_ID)
     pl.semaphore_signal(barrier, inc=1, device_id=(me, other), device_id_type=MESH_ID)
-    for fetch in fetches[4:]:
+    for fetch in fetches[4:8]:
         fetch.start()
+
+    def greet(step):
+        for to in (me + 2**step, me + gz_count - 2**step):
+            pl.semaphore_signal(
+                known_sem.at[step],
+                inc=1,
+                device_id=(lax.rem(to, gz_count), ph),
+                device_id_type=MESH_ID,
+            )
+
+    steps = known_sem.shape[0]
+
+    def spread(step):
+        if step < steps:
+            pl.semaphore_wait(known_sem.at[step], 2)
+        if step + 1 < steps:
+            greet(step + 1)
 
     radii = lax.broadcasted_iota(jnp.int32, (rows, around), 0).astype(jnp.float32) + 0.5
     row_id = lax.broadcasted_iota(jnp.int32, (rows, around), 0)
     lane = lax.broadcasted_iota(jnp.int32, (rows, half), 1)
 
-    fetches[0].wait()
-
     def rotate(z):
         turn = offsets_ref[lax.rem(me * planes + z, axial_total)]
         fluid[z] = pltpu.roll(wall_ref[...].astype(jnp.float32), turn, 1)
 
+    for fetch in fetches[:4]:
+        fetch.wait()
     rotate(planes)
-    for fetch in fetches[1:4]:
-        fetch.wait()
     size = diameters_ref[map_ref[0]]
 
     arc = 1.0 / (radii * angle_step)
@@ -374,9 +394,11 @@
         modes[1, z] = out[:, half:]
         swap(z).start()
 
-    axial_flux[...] = source(planes - 1)
-    fetches[4].wait()
-    pl.semaphore_wait(barrier, gz_count)
+    axial_flux[...] = source(last)
+    for fetch in fetches[8:]:
+        fetch.start()
+    pl.semaphore_wait(barrier, 3)
+    greet(0)
     halo_copy = pltpu.make_async_remote_copy(
         src_ref=axial_flux,
         dst_ref=halo,
@@ -386,6 +408,8 @@
         device_id_type=MESH_ID,
     )
     halo_copy.start()
+    for fetch in fetches[4:8]:
+        fetch.wait()
 
     def send_modes(k, carry):
         z = planes - 2 - k
@@ -396,7 +420,8 @@
     halo_copy.wait()
     to_modes(0, halo[...])
 
-    for fetch in fetches[5:]:
+    spread(0)
+    for fetch in fetches[8:]:
         fetch.wait()
 
     def apply(table, loads):
@@ -422,7 +447,11 @@
         lines[ph, z] = jnp.where(lane + other == 0, exact, out)
         return carry
 
-    lax.fori_loop(0, planes, forward, 0)
+    lax.fori_loop(0, planes // 2, forward, 0)
+    spread(1)
+    lax.fori_loop(planes // 2, planes, forward, 0)
+    for step in range(2, steps):
+        spread(step)
 
     ratio = line_ref[ph, 0]
     rising = lines[ph, 0]
@@ -482,7 +511,8 @@
     late = me // (gz_count // 2)
 
     for k in range(owners):
-        o = lax.rem(k + (1 - late) * blocks, owners)
+        side = 1 - late if k < blocks else late
+        o = side * blocks + lax.rem(k + me, blocks)
 
         @pl.when(base + o != me)
         def _(o=o):
@@ -553,20 +583,20 @@
             solved[z] = (solved[z] + left) * scale
         solved[planes] = (last + left * ratio) * scale
 
-    groups = (planes + 1) // group
-
-    def inverse(h, k):
-        loads = [lambda r, z=k * group + i: solved[z, pl.ds(r, 1), :] for i in range(group)]
-        return apply(radial_back.at[h], loads)
+    left_over = list(range(planes + 1))
+    groups = []
+    while left_over:
+        groups.append(left_over[-4:])
+        left_over = left_over[:-4]
+
+    def inverse(h, at):
+        return apply(radial_back.at[h], [lambda r, z=z: solved[z, pl.ds(r, 1), :] for z in at])
 
     solve(ph)
 
-    def own_half(k, carry):
-        for i, out in enumerate(inverse(ph, k)):
-            result[k * group + i] = out
-        return carry
-
-    lax.fori_loop(0, groups, own_half, 0)
+    for at in groups:
+        for z, out in zip(at, inverse(ph, at)):
+            result[z] = out
 
     share_lines.wait_recv()
     sent_relay.wait_recv()
@@ -581,17 +611,19 @@
         for a, step in enumerate((radial_step, around_step, axial_step)):
             corrected_ref[0, a, z] = (pred[a, z] - step).astype(jnp.bfloat16)
 
-    for k in range(groups):
-        outs = inverse(other, k)
-        own = jnp.concatenate([result[k * group + i] for i in range(group)], 0)
+    before = []
+    for at in groups:
+        outs = inverse(other, at)
+        own = jnp.concatenate([result[z] for z in at], 0)
         both = jnp.concatenate([own, jnp.concatenate(outs, 0)], 1)
         table = [jnp.concatenate([back_ref[i, ph], back_ref[i, other]], 0) for i in range(2)]
         found = triple_dot(both, *table)
-        for z in range(max((k - 1) * group - 1, 0), k * group - 1):
+        for z in before:
             correct(z)
-        for i in range(group):
-            space[k * group + i] = found[i * rows : (i + 1) * rows]
-    for z in range(max((groups - 1) * group - 1, 0), planes):
+        for i, z in enumerate(at):
+            space[z] = found[i * rows : (i + 1) * rows]
+        before = [z for z in at if z < planes]
+    for z in before:
         correct(z)
 
     whole(modes.at[other], swap_send, swap_recv.at[0]).wait_send()
@@ -610,12 +642,13 @@
 
 
 def put_kernel(pressure_vmem, corrected_vmem, pressure_out, corrected_out, sem):
-    pairs = ((pressure_vmem, pressure_out), (corrected_vmem, corrected_out))
-    copies = [pltpu.make_async_copy(a, b, sem.at[i]) for i, (a, b) in enumerate(pairs)]
-    for copy in copies:
-        copy.start()
-    for copy in copies:
-        copy.wait()
+    planes = pressure_vmem.shape[0]
+    for z in range(planes):
+        pltpu.make_async_copy(pressure_vmem.at[z], pressure_out.at[z], sem.at[0]).start()
+        at = (0, slice(None), z)
+        pltpu.make_async_copy(corrected_vmem.at[at], corrected_out.at[at], sem.at[1]).start()
+    pltpu.make_async_copy(pressure_vmem, pressure_out, sem.at[0]).wait()
+    pltpu.make_async_copy(corrected_vmem, corrected_out, sem.at[1]).wait()
 
 
 def drum_step(gz_count, frac, velocity, gas_vel, diameters, phase_map, wall_mask, offsets):
@@ -627,9 +660,8 @@
     dma = pltpu.SemaphoreType.DMA
     owners = gz_count // 2
     width = 2 * rows // owners
-    group = 3 if (planes + 1) % 3 == 0 else 1
     results = pl.pallas_call(
-        functools.partial(drum_kernel, gz_count, group),
+        functools.partial(drum_kernel, gz_count),
         out_shape=(
             pltpu.VMEM((planes, rows, around), f32),
             pltpu.VMEM((1, 3, planes, rows, around), jnp.bfloat16),
@@ -664,7 +696,7 @@
             pltpu.VMEM((planes + 1, rows, half), f32),
             pltpu.VMEM((planes + 1, rows, half), f32),
             pltpu.VMEM((planes + 1, rows, around), f32),
-            dma((10,)),
+            dma((13,)),
             dma((2,)),
             dma,
             dma((planes,)),
@@ -673,6 +705,7 @@
             dma,
             dma((owners,)),
             dma((2,)),
+            pltpu.SemaphoreType.REGULAR(((gz_count // 2 - 1).bit_length(),)),
         ],
         compiler_params=pltpu.CompilerParams(
             collective_id=0, has_side_effects=True, vmem_limit_bytes=56 * 1024 * 1024

time: 31 us -> 29.9 us (0.965)
  Pallas kernels: 29.5 us -> 28.4 us
    pallas_call x1, Pallas kernels: 28.4 us -> 27.3 us  [drum_step(): pl.pallas_call(functools.partial(drum_kernel, gz_count), out_shape=(pltpu...]
where the time goes in v4:
time: 29.9 us; the launch traced here: 29.7 us
  Pallas kernels  28.4 us (95%)
  between operations  1.29 us (4%)
    pallas_call x1, Pallas kernels, drum_step(): pl.pallas_call(functools.partial(drum_kernel, gz_count), out_shape=(pltpu...  27.3 us
    pallas_call x1, Pallas kernels, drum_step(): pl.pallas_call(put_kernel, out_shape=tuple((jax.ShapeDtypeStruct(x.shape,...  1.05 us

profile of v4, /device:TPU:0, one launch (start us, length us, event | category | flops | bytes accessed | tf_op | source)
XLA Modules:
  0.0 29.7 jit_solution(5011281289490897601)
XLA Ops:
  1.3 27.3 %shard_map.140 = (f32[8,64,256]{2,1,0:T(8,128)S(1)}, bf16[1,3,8,64,256]{4,3,2,1,0:T(8,128)(2,1)S(1)}) custom-call(s32[128]{0:T(128)} %offsets_ref.1, f32[32]{0:T(128)} %diameters_ref.1, s32[1]{0:T(128)S(6)} %copy.15.map_ref, s32[64,256]{1,0:T(8,128)} %wall_hbm.1, bf16[1,8,64,256]{3,2,1,0:T(8,128)(2,1)} %frac_hbm.1, bf16[1,3,8,64,256]{4,3,2,1,0:T(8,128)(2,1)} %velocity_hbm.1, ...), custom_call_target="tpu_custom_call" | custom-call | tf_op jit(solution)/shard_map/pallas_call | solution.py:663
  28.6 1.1 %shard_map.141 = (f32[8,64,256]{2,1,0:T(8,128)}, bf16[1,3,8,64,256]{4,3,2,1,0:T(8,128)(2,1)}) custom-call(f32[8,64,256]{2,1,0:T(8,128)S(1)} %get-tuple-element.4.pressure_vmem, bf16[1,3,8,64,256]{4,3,2,1,0:T(8,128)(2,1)S(1)} %get-tuple-element.5.corrected_vmem), custom_call_target="tpu_custom_call" | custom-call | tf_op jit(solution)/shard_map/pallas_call | solution.py:728

commit v5 on v4

--- a/solution.py
+++ b/solution.py
@@ -218,9 +218,9 @@
 
 def drum_kernel(
     gz_count,
-    offsets_ref,
-    diameters_ref,
-    map_ref,
+    offsets_hbm,
+    diameters_hbm,
+    map_hbm,
     wall_hbm,
     frac_hbm,
     velocity_hbm,
@@ -233,6 +233,9 @@
     radial_hbm,
     pressure_ref,
     corrected_ref,
+    offsets_ref,
+    diameters_ref,
+    map_ref,
     wall_ref,
     frac_ref,
     velocity_ref,
@@ -260,6 +263,7 @@
     solved,
     result,
     space,
+    scalar_sem,
     input_sem,
     halo_sem,
     swap_send,
@@ -303,8 +307,10 @@
     pairs += [(part(a, 0, last), part(b, 0, last)) for a, b in streams]
     pairs += tables
     fetches = [pltpu.make_async_copy(a, b, input_sem.at[i]) for i, (a, b) in enumerate(pairs)]
+    small = ((offsets_hbm, offsets_ref), (diameters_hbm, diameters_ref), (map_hbm, map_ref))
+    scalars = [pltpu.make_async_copy(a, b, scalar_sem.at[i]) for i, (a, b) in enumerate(small)]
     barrier = pltpu.get_barrier_semaphore()
-    for fetch in fetches[:4]:
+    for fetch in scalars + fetches[:4]:
         fetch.start()
     for to in ((lax.rem(me + 1, gz_count), ph), (lax.rem(me + gz_count - 1, gz_count), ph)):
         pl.semaphore_signal(barrier, inc=1, device_id=to, device_id_type=MESH_ID)
@@ -337,7 +343,7 @@
         turn = offsets_ref[lax.rem(me * planes + z, axial_total)]
         fluid[z] = pltpu.roll(wall_ref[...].astype(jnp.float32), turn, 1)
 
-    for fetch in fetches[:4]:
+    for fetch in scalars + fetches[:4]:
         fetch.wait()
     rotate(planes)
     size = diameters_ref[map_ref[0]]
@@ -655,7 +661,6 @@
     planes, rows, around = frac.shape[1:]
     half = around // 2
     first, nyquist, fill, line, ahead, back = operator_tables(rows, around, offsets.shape[0], planes)
-    smem = pl.BlockSpec(memory_space=pltpu.SMEM)
     f32 = jnp.float32
     dma = pltpu.SemaphoreType.DMA
     owners = gz_count // 2
@@ -666,9 +671,12 @@
             pltpu.VMEM((planes, rows, around), f32),
             pltpu.VMEM((1, 3, planes, rows, around), jnp.bfloat16),
         ),
-        in_specs=[smem] * 3 + [pl.BlockSpec(memory_space=pl.ANY)] * 10,
+        in_specs=[pl.BlockSpec(memory_space=pl.ANY)] * 13,
         out_specs=[pl.BlockSpec(memory_space=pltpu.VMEM)] * 2,
         scratch_shapes=[
+            pltpu.SMEM(offsets.shape, jnp.int32),
+            pltpu.SMEM(diameters.shape, f32),
+            pltpu.SMEM(phase_map.shape, jnp.int32),
             pltpu.VMEM(wall_mask.shape, jnp.int32),
             pltpu.VMEM(frac.shape, jnp.bfloat16),
             pltpu.VMEM(velocity.shape, jnp.bfloat16),
@@ -696,6 +704,7 @@
             pltpu.VMEM((planes + 1, rows, half), f32),
             pltpu.VMEM((planes + 1, rows, half), f32),
             pltpu.VMEM((planes + 1, rows, around), f32),
+            dma((3,)),
             dma((13,)),
             dma((2,)),
             dma,

time: 29.9 us -> 29.2 us (0.977)
  Pallas kernels: 28.4 us -> 27.7 us
    pallas_call x1, Pallas kernels: 27.3 us -> 26.7 us  [drum_step(): pl.pallas_call(functools.partial(drum_kernel, gz_count), out_shape=(pltpu...]
where the time goes in v5:
time: 29.2 us; the launch traced here: 29 us
  Pallas kernels  27.7 us (95%)
  between operations  1.29 us (4%)
    pallas_call x1, Pallas kernels, drum_step(): pl.pallas_call(functools.partial(drum_kernel, gz_count), out_shape=(pltpu...  26.7 us
    pallas_call x1, Pallas kernels, drum_step(): pl.pallas_call(put_kernel, out_shape=tuple((jax.ShapeDtypeStruct(x.shape,...  1.05 us

profile of v5, /device:TPU:0, one launch (start us, length us, event | category | flops | bytes accessed | tf_op | source)
XLA Modules:
  0.0 29.0 jit_solution(2476061981122303182)
XLA Ops:
  1.3 26.7 %shard_map.140 = (f32[8,64,256]{2,1,0:T(8,128)S(1)}, bf16[1,3,8,64,256]{4,3,2,1,0:T(8,128)(2,1)S(1)}) custom-call(s32[128]{0:T(128)} %offsets_hbm.1, f32[32]{0:T(128)} %diameters_hbm.1, s32[1]{0:T(128)S(6)} %copy.15.map_hbm, s32[64,256]{1,0:T(8,128)} %wall_hbm.1, bf16[1,8,64,256]{3,2,1,0:T(8,128)(2,1)} %frac_hbm.1, bf16[1,3,8,64,256]{4,3,2,1,0:T(8,128)(2,1)} %velocity_hbm.1, ...), custom_call_target="tpu_custom_call" | custom-call | tf_op jit(solution)/shard_map/pallas_call | solution.py:668
  28.0 1.1 %shard_map.141 = (f32[8,64,256]{2,1,0:T(8,128)}, bf16[1,3,8,64,256]{4,3,2,1,0:T(8,128)(2,1)}) custom-call(f32[8,64,256]{2,1,0:T(8,128)S(1)} %get-tuple-element.4.pressure_vmem, bf16[1,3,8,64,256]{4,3,2,1,0:T(8,128)(2,1)S(1)} %get-tuple-element.5.corrected_vmem), custom_call_target="tpu_custom_call" | custom-call | tf_op jit(solution)/shard_map/pallas_call | solution.py:737

commit v6 on v5

--- a/solution.py
+++ b/solution.py
@@ -262,6 +262,7 @@
     states_in,
     solved,
     result,
+    result_other,
     space,
     scalar_sem,
     input_sem,
@@ -285,6 +286,8 @@
     base = gz_count // 4
     width = ends_in.shape[1]
     blocks = owners // 2
+    pair = blocks // 2
+    half_rows = rows // 2
     angle_step = 2.0 * math.pi / around
 
     last = planes - 1
@@ -430,18 +433,19 @@
     for fetch in fetches[8:]:
         fetch.wait()
 
-    def apply(table, loads):
+    def apply(table, loads, start=0, count=rows, accs=None):
         def add(k, accs):
             accs = list(accs)
             for j in range(8):
-                r = k * 8 + j
+                r = start + k * 8 + j
                 part = table[pl.ds(pl.multiple_of(r * rows, rows), rows), :]
                 for i, load in enumerate(loads):
                     accs[i] = accs[i] + part * jnp.broadcast_to(load(r), (rows, half))
             return tuple(accs)
 
-        zero = jnp.zeros((rows, half), jnp.float32)
-        return lax.fori_loop(0, rows // 8, add, (zero,) * len(loads))
+        if accs is None:
+            accs = (jnp.zeros((rows, half), jnp.float32),) * len(loads)
+        return lax.fori_loop(0, count // 8, add, tuple(accs))
 
     def forward(k, carry):
         z = planes - 1 - k
@@ -467,8 +471,9 @@
     for z in range(planes - 2, -1, -1):
         falling = falling * ratio + lines[ph, z]
     for j in range(blocks):
-        ends_out[j] = rising[width * j : width * j + width]
-        ends_out[blocks + j] = falling[width * j : width * j + width]
+        o = j // pair * blocks + j % pair
+        ends_out[o] = rising[width * j : width * j + width]
+        ends_out[o + pair] = falling[width * j : width * j + width]
 
     is_owner = (me >= base) & (me < base + owners)
 
@@ -497,7 +502,7 @@
             src_ref=states_in.at[h, at],
             dst_ref=states_in.at[h, at],
             send_sem=relay_sem.at[0],
-            recv_sem=relay_sem.at[1],
+            recv_sem=relay_sem.at[1 + at // blocks],
             device_id=(me, other),
             device_id_type=MESH_ID,
         )
@@ -513,7 +518,11 @@
         )
 
     sent_ends = whole(ends_in.at[pl.ds(0, gz_count - 1)], ends_sem.at[0], ends_sem.at[1])
-    sent_relay = whole(states_in.at[other], relay_sem.at[0], relay_sem.at[1])
+
+    def relayed(side):
+        part = states_in.at[other, pl.ds(side * blocks, blocks)]
+        return whole(part, relay_sem.at[0], relay_sem.at[1 + side])
+
     late = me // (gz_count // 2)
 
     for k in range(owners):
@@ -544,8 +553,9 @@
     def _():
         sent_ends.wait_recv()
         mine = me - base
-        is_rise = 1 - mine // blocks
-        at = pl.ds(pl.multiple_of(lax.rem(mine, blocks) * width, width), width)
+        is_rise = 1 - lax.rem(mine, blocks) // pair
+        block = mine // blocks * pair + lax.rem(mine, pair)
+        at = pl.ds(pl.multiple_of(block * width, width), width)
         jump = line_ref[ph, 2, at, :]
         wrap = line_ref[ph, 3, at, :]
         order = [is_rise * s + (1 - is_rise) * (gz_count - 1 - s) for s in range(gz_count)]
@@ -565,29 +575,32 @@
         fill = jnp.broadcast_to(fill_ref[:, l : l + 1], (rows, half))
         radial_back[1, at, :] = jnp.where(lane == 0, fill, radial_back[0, at, :])
 
-    for k in range(owners):
-        o = lax.rem(k + late * blocks, owners)
-
-        @pl.when(base + o != me)
-        def _(o=o):
-            give_states(me, o).wait_recv()
-
-        relay(o, ph).start()
-
-    def solve(h):
-        ratio = line_ref[h, 0]
-        scale = line_ref[h, 1]
-        right = jnp.concatenate([states_in[h, blocks + j] for j in range(blocks)], 0)
-        left = jnp.concatenate([states_in[h, j] for j in range(blocks)], 0)
-        last = right
+    def collect(side):
+        for k in range(blocks):
+            o = side * blocks + k
+
+            @pl.when(base + o != me)
+            def _(o=o):
+                give_states(me, o).wait_recv()
+
+            relay(o, ph).start()
+
+    def solve(h, side):
+        at = pl.ds(pl.multiple_of(side * half_rows, 8), half_rows)
+        ratio = line_ref[h, 0, at, :]
+        scale = line_ref[h, 1, at, :]
+        states = [states_in[h, side * blocks + k] for k in range(blocks)]
+        left = jnp.concatenate(states[:pair], 0)
+        right = jnp.concatenate(states[pair:], 0)
         behind = right * ratio
+        back = [None] * planes
         for z in range(planes - 1, -1, -1):
-            solved[z] = behind
-            behind = (behind + lines[h, z]) * ratio
+            back[z] = behind
+            behind = (behind + lines[h, z, at, :]) * ratio
         for z in range(planes):
-            left = left * ratio + lines[h, z]
-            solved[z] = (solved[z] + left) * scale
-        solved[planes] = (last + left * ratio) * scale
+            left = left * ratio + lines[h, z, at, :]
+            solved[z, at, :] = (back[z] + left) * scale
+        solved[planes, at, :] = (right + left * ratio) * scale
 
     left_over = list(range(planes + 1))
     groups = []
@@ -595,18 +608,29 @@
         groups.append(left_over[-4:])
         left_over = left_over[:-4]
 
-    def inverse(h, at):
-        return apply(radial_back.at[h], [lambda r, z=z: solved[z, pl.ds(r, 1), :] for z in at])
-
-    solve(ph)
-
+    def inverse(h, at, side, accs):
+        loads = [lambda r, z=z: solved[z, pl.ds(r, 1), :] for z in at]
+        return apply(radial_back.at[h], loads, side * half_rows, half_rows, accs)
+
+    def near_half(h, to):
+        solve(h, late)
+        for at in groups:
+            for z, out in zip(at, inverse(h, at, late, None)):
+                to[z] = out
+
+    collect(late)
+    near_half(ph, result)
+    collect(1 - late)
+    solve(ph, 1 - late)
     for at in groups:
-        for z, out in zip(at, inverse(ph, at)):
+        for z, out in zip(at, inverse(ph, at, 1 - late, [result[z] for z in at])):
             result[z] = out
 
     share_lines.wait_recv()
-    sent_relay.wait_recv()
-    solve(other)
+    relayed(late).wait_recv()
+    near_half(other, result_other)
+    relayed(1 - late).wait_recv()
+    solve(other, 1 - late)
 
     def correct(z):
         here = space[z]
@@ -619,7 +643,7 @@
 
     before = []
     for at in groups:
-        outs = inverse(other, at)
+        outs = inverse(other, at, 1 - late, [result_other[z] for z in at])
         own = jnp.concatenate([result[z] for z in at], 0)
         both = jnp.concatenate([own, jnp.concatenate(outs, 0)], 1)
         table = [jnp.concatenate([back_ref[i, ph], back_ref[i, other]], 0) for i in range(2)]
@@ -634,7 +658,7 @@
 
     whole(modes.at[other], swap_send, swap_recv.at[0]).wait_send()
     share_lines.wait_send()
-    sent_relay.wait_send()
+    whole(states_in.at[other], relay_sem.at[0], relay_sem.at[1]).wait_send()
 
     @pl.when(is_owner)
     def _():
@@ -703,6 +727,7 @@
             pltpu.VMEM((2, owners, width, half), f32),
             pltpu.VMEM((planes + 1, rows, half), f32),
             pltpu.VMEM((planes + 1, rows, half), f32),
+            pltpu.VMEM((planes + 1, rows, half), f32),
             pltpu.VMEM((planes + 1, rows, around), f32),
             dma((3,)),
             dma((13,)),
@@ -713,7 +738,7 @@
             dma((2,)),
             dma,
             dma((owners,)),
-            dma((2,)),
+            dma((3,)),
             pltpu.SemaphoreType.REGULAR(((gz_count // 2 - 1).bit_length(),)),
         ],
         compiler_params=pltpu.CompilerParams(
@@ -759,7 +784,7 @@
 
     def body(frac, *rest):
         rows, around = frac.shape[2:]
-        fits = ph_count == 2 and around == 256 and rows <= 128 and gz_count % 4 == 0
+        fits = ph_count == 2 and around == 256 and rows <= 128 and gz_count % 8 == 0
         if fits and rows * 2 == gz_count * 8 and frac.shape[1] <= 8:
             return drum_step(gz_count, frac, *rest)
         return shards(frac, *rest)

time: 29.2 us -> 28.7 us (0.983)
  Pallas kernels: 27.7 us -> 27.2 us
    pallas_call x1, Pallas kernels: 26.7 us -> 26.1 us  [drum_step(): pl.pallas_call(functools.partial(drum_kernel, gz_count), out_shape=(pltpu...]
where the time goes in v6:
time: 28.7 us; the launch traced here: 28.5 us
  Pallas kernels  27.2 us (95%)
  between operations  1.29 us (4%)
    pallas_call x1, Pallas kernels, drum_step(): pl.pallas_call(functools.partial(drum_kernel, gz_count), out_shape=(pltpu...  26.1 us
    pallas_call x1, Pallas kernels, drum_step(): pl.pallas_call(put_kernel, out_shape=tuple((jax.ShapeDtypeStruct(x.shape,...  1.05 us

profile of v6, /device:TPU:0, one launch (start us, length us, event | category | flops | bytes accessed | tf_op | source)
XLA Modules:
  0.0 28.5 jit_solution(3438202508001671556)
XLA Ops:
  1.3 26.1 %shard_map.140 = (f32[8,64,256]{2,1,0:T(8,128)S(1)}, bf16[1,3,8,64,256]{4,3,2,1,0:T(8,128)(2,1)S(1)}) custom-call(s32[128]{0:T(128)} %offsets_hbm.1, f32[32]{0:T(128)} %diameters_hbm.1, s32[1]{0:T(128)S(6)} %copy.15.map_hbm, s32[64,256]{1,0:T(8,128)} %wall_hbm.1, bf16[1,8,64,256]{3,2,1,0:T(8,128)(2,1)} %frac_hbm.1, bf16[1,3,8,64,256]{4,3,2,1,0:T(8,128)(2,1)} %velocity_hbm.1, ...), custom_call_target="tpu_custom_call" | custom-call | tf_op jit(solution)/shard_map/pallas_call | solution.py:692
  27.4 1.1 %shard_map.141 = (f32[8,64,256]{2,1,0:T(8,128)}, bf16[1,3,8,64,256]{4,3,2,1,0:T(8,128)(2,1)}) custom-call(f32[8,64,256]{2,1,0:T(8,128)S(1)} %get-tuple-element.4.pressure_vmem, bf16[1,3,8,64,256]{4,3,2,1,0:T(8,128)(2,1)S(1)} %get-tuple-element.5.corrected_vmem), custom_call_target="tpu_custom_call" | custom-call | tf_op jit(solution)/shard_map/pallas_call | solution.py:762
